TPU v7x, 32 devices: a whole 2x2x4 slice. The times are simulated.
32 devices in a mesh: fsdp: 4 (over z), ctx: 2 (over y), tp: 4 (over x, core).
Axes of the slice: x: 2, y: 2, z: 4, core: 2. Of those that a mesh axis runs over, the one named last changes fastest.
Arguments:
- tokens: bfloat16 [1024, 768], P(('fsdp', 'ctx')), may hold values from -6 to 6
- segments: int32 [4, 256], P('fsdp'), may hold values from 0 to 3, never falling along the last dimension, each value on 1 to 128 neighbouring positions
- cotangent: float32 [1024, 768], P(('fsdp', 'ctx')), may hold values from -6 to 6
- prenorm: float32 [2, 768], replicated, may hold values from 0.5 to 1.5
- gate_proj: bfloat16 [2, 768, 1536], P(None, ('fsdp', 'ctx'), 'tp'), may hold values from -0.21875 to 0.21875
- inner_proj: bfloat16 [2, 768, 1536], P(None, ('fsdp', 'ctx'), 'tp'), may hold values from -0.21875 to 0.21875
- state_proj: bfloat16 [2, 768, 256], P(None, ('fsdp', 'ctx')), may hold values from -0.21875 to 0.21875
- step_proj: bfloat16 [2, 768, 24], P(None, ('fsdp', 'ctx'), 'tp'), may hold values from -0.21875 to 0.21875
- inner_kernel: float32 [2, 4, 1536], P(None, None, 'tp'), may hold values from -3 to 3
- inner_offset: float32 [2, 1536], P(None, 'tp'), may hold values from -3 to 3
- state_kernel: float32 [2, 4, 256], replicated, may hold values from -3 to 3
- state_offset: float32 [2, 256], replicated, may hold values from -3 to 3
- step_bias: float32 [2, 24], P(None, 'tp'), may hold values from -7 to -3
- decay_log: float32 [2, 24], P(None, 'tp'), may hold values from -3 to 1
- skip_gain: float32 [2, 24], P(None, 'tp'), may hold values from 0.5 to 1.5
- norm_gain: float32 [2, 1536], P(None, 'tp'), may hold values from 0.5 to 1.5
- mixer_out: bfloat16 [2, 768, 1536], P(None, ('fsdp', 'ctx'), 'tp'), may hold values from -0.15625 to 0.15625
Outputs:
- output: float32 [1024, 768], P(('fsdp', 'ctx'), 'tp')
- token_grad: float32 [1024, 768], P(('fsdp', 'ctx'), 'tp')
- prenorm_grad: float32 [2, 768], P(None, 'tp')
- gate_grad: float32 [2, 768, 1536], P(None, ('fsdp', 'ctx'), 'tp')
- inner_grad: float32 [2, 768, 1536], P(None, ('fsdp', 'ctx'), 'tp')
- state_grad: float32 [2, 768, 256], P(None, ('fsdp', 'ctx'))
- step_grad: float32 [2, 768, 24], P(None, ('fsdp', 'ctx'), 'tp')
- inner_kernel_grad: float32 [2, 4, 1536], P(None, None, 'tp')
- inner_offset_grad: float32 [2, 1536], P(None, 'tp')
- state_kernel_grad: float32 [2, 4, 256], replicated
- state_offset_grad: float32 [2, 256], replicated
- step_bias_grad: float32 [2, 24], P(None, 'tp')
- decay_log_grad: float32 [2, 24], P(None, 'tp')
- skip_gain_grad: float32 [2, 24], P(None, 'tp')
- norm_gain_grad: float32 [2, 1536], P(None, 'tp')
- mixer_grad: float32 [2, 768, 1536], P(None, ('fsdp', 'ctx'), 'tp')
Inputs may be any that keep to these rules, and one draw needn't show every extreme that they name: `segments`: each row holds one token run; its segment numbers never fall, each sequence holds 1 to 128 tokens, and one holds exactly 128.
All inputs are finite; a program needn't handle non-finite values.
Results may differ from a plain program's by a relative error of at most 0.017.
Values may be sent and summed in bfloat16 or wider, within the bound.
A program may use at most 128 MiB of HBM per device.

v0:
```python
import jax
import jax.numpy as jnp
from jax import lax
from jax.sharding import PartitionSpec as P

SPAN = 128


EPSILON = 1e-05
HIGH = lax.Precision.HIGHEST


def passed_along(block, axis, distance):
    devices = range(lax.axis_size(axis))
    route = [(i - distance, i) for i in devices if i - distance in devices]
    return lax.ppermute(block, axis, route)


def prefix(shard, axis, join, neutral):
    place = lax.axis_index(axis)
    gathered = jax.tree.map(
        lambda a, kind: lax.all_gather(a.astype(kind), axis), shard, (jnp.bfloat16, jnp.bfloat16)
    )
    state = jax.tree.map(lambda a, e: jnp.zeros_like(a) + jnp.asarray(e, a.dtype), shard, neutral)

    def prefix_one(turn, state):
        return join(
            state,
            jax.tree.map(
                lambda a, own: lax.dynamic_index_in_dim(a, turn, 0, False).astype(own.dtype),
                gathered,
                shard,
            ),
        )

    return lax.fori_loop(0, place, prefix_one, state)


def entering(shard, axis, join, neutral):
    count = lax.axis_size(axis)
    place = lax.axis_index(axis)
    ahead = count - 1 - place
    gathered = jax.tree.map(
        lambda a, kind: lax.all_gather(a.astype(kind), axis),
        shard,
        jax.tree.map(lambda a: jnp.bfloat16 if a.dtype == jnp.float32 else a.dtype, shard),
    )
    state = jax.tree.map(lambda a, e: jnp.zeros_like(a) + jnp.asarray(e, a.dtype), shard, neutral)

    def entering_one(turn, state):
        source = count - 1 - turn
        return join(
            state,
            jax.tree.map(
                lambda a, own: lax.dynamic_index_in_dim(a, source, 0, False).astype(own.dtype),
                gathered,
                shard,
            ),
        )

    return lax.fori_loop(0, ahead, entering_one, state)


def rms_apply(hidden, gain):
    inverse = lax.rsqrt(jnp.mean(hidden * hidden, axis=-1, keepdims=True) + EPSILON)
    return hidden * inverse * gain


def conv_apply(padded, seg_padded, kernel, offset):
    taps = kernel.shape[0]
    length = padded.shape[0] - taps + 1
    current = seg_padded[taps - 1 :]
    total = jnp.zeros((length, padded.shape[1]), jnp.float32) + offset
    for shift_index in range(taps):
        same = (seg_padded[shift_index : shift_index + length] == current).astype(jnp.float32)
        total = (
            total + kernel[shift_index] * padded[shift_index : shift_index + length] * same[:, None]
        )
    return jax.nn.silu(total)


def fresh_flags(seg, cont):
    first = jnp.reshape(1.0 - cont, (1,))
    return jnp.concatenate([first, (seg[1:] != seg[:-1]).astype(jnp.float32)])


def inflow(step, decay, seg, cont):
    alive = (jnp.cumsum(fresh_flags(seg, cont)) == 0.0).astype(jnp.float32)
    return alive[:, None] * jnp.exp(jnp.cumsum(step * decay[None, :], axis=0))


def ssd_block(inner, bmat, cmat, step, decay, skip, seg, cont, carry_in):
    length, heads, head_size = inner.shape
    blocks = length // SPAN
    fresh = fresh_flags(seg, cont)

    def advance(carry, piece):
        part_x, part_b, part_c, part_dt, part_seg, part_fresh = piece
        logs = jnp.cumsum(part_dt * decay[None, :], axis=0)
        order = jnp.arange(SPAN)
        allowed = (order[:, None] >= order[None, :]) & (part_seg[:, None] == part_seg[None, :])
        gap = logs[:, None, :] - logs[None, :, :]
        weights = jnp.where(
            allowed[:, :, None], jnp.exp(jnp.where(allowed[:, :, None], gap, 0.0)), 0.0
        )
        scores = jnp.dot(part_c, part_b.T, precision=HIGH)
        scaled = part_x * part_dt[:, :, None]
        local = jnp.einsum("tsh,shp->thp", weights * scores[:, :, None], scaled, precision=HIGH)
        alive = (jnp.cumsum(part_fresh) == 0.0).astype(jnp.float32)
        into = alive[:, None] * jnp.exp(logs)
        carried = into[:, :, None] * jnp.einsum("tn,hpn->thp", part_c, carry, precision=HIGH)
        tail = (
            jnp.exp(logs[-1][None, :] - logs)
            * (part_seg == part_seg[-1]).astype(jnp.float32)[:, None]
        )
        update = jnp.einsum("shp,sn->hpn", scaled * tail[:, :, None], part_b, precision=HIGH)
        return (into[-1][:, None, None] * carry + update, local + carried)

    pieces = (
        inner.reshape(blocks, SPAN, heads, head_size),
        bmat.reshape(blocks, SPAN, -1),
        cmat.reshape(blocks, SPAN, -1),
        step.reshape(blocks, SPAN, heads),
        seg.reshape(blocks, SPAN),
        fresh.reshape(blocks, SPAN),
    )
    final, outputs = lax.scan(advance, carry_in, pieces)
    return (outputs.reshape(length, heads, head_size) + skip[None, :, None] * inner, final)


def link(earlier, later):
    return (earlier[0] * later[0], later[0][:, None, None] * earlier[1] + later[1])


def contract_cols(left, right):
    return lax.dot_general(
        left, right, (((1,), (1,)), ((), ())), preferred_element_type=jnp.float32
    )


def project(normed, weight, feat_dim):
    return lax.dot_general(
        normed, weight, (((feat_dim,), (0,)), ((), ())), preferred_element_type=jnp.float32
    )


def grad_rows(normed, delta, feat_dim):
    return lax.dot_general(
        normed, delta, (((1 - feat_dim,), (0,)), ((), ())), preferred_element_type=jnp.float32
    )


def body(
    tokens,
    segments,
    cotangent,
    prenorm,
    gate_proj,
    inner_proj,
    state_proj,
    step_proj,
    inner_kernel,
    inner_offset,
    state_kernel,
    state_offset,
    step_bias,
    decay_log,
    skip_gain,
    norm_gain,
    mixer_out,
):
    length = tokens.shape[0]
    model = tokens.shape[1]
    layers = gate_proj.shape[0]
    taps = inner_kernel.shape[1]
    inner_local = gate_proj.shape[2]
    heads_local = step_proj.shape[2]
    head_size = inner_local // heads_local
    state_size = state_proj.shape[2] // 2
    inner_all = inner_local * lax.axis_size("tp")
    feat = model // lax.axis_size("tp")
    feat_start = lax.axis_index("tp") * feat
    start = lax.axis_index("ctx") * length
    seg_pad = jnp.concatenate([jnp.full((taps - 1,), -1, jnp.int32), segments[0]])
    seg_padded = lax.dynamic_slice_in_dim(seg_pad, start, length + taps - 1)
    seg_here = seg_padded[taps - 1 :]
    cont = (seg_padded[taps - 2] == seg_padded[taps - 1]).astype(jnp.float32)
    zeros_state = jnp.zeros((heads_local, head_size, state_size), jnp.float32)
    identity = (jnp.ones((heads_local,), jnp.float32), zeros_state)

    def layer_kernel(layer):
        kernel = jnp.concatenate([inner_kernel[layer], state_kernel[layer]], 1)
        offset = jnp.concatenate([inner_offset[layer], state_offset[layer]])
        return (kernel, offset)

    def split_act(act, layer):
        inner = act[:, :inner_local].reshape(length, heads_local, head_size)
        bmat = act[:, inner_local : inner_local + state_size]
        cmat = act[:, inner_local + state_size :]
        step = jax.nn.softplus(kept_step[layer] + step_bias[layer])
        return (inner, bmat, cmat, step)

    feat_dim = 1
    hidden = tokens.astype(jnp.float32)
    back = cotangent
    kept = []
    kept_step = []
    for layer in range(layers):
        mats = (
            lax.all_gather(gate_proj[layer], ("fsdp", "ctx"), axis=0, tiled=True),
            lax.all_gather(inner_proj[layer], ("fsdp", "ctx"), axis=0, tiled=True),
            lax.all_gather(state_proj[layer], ("fsdp", "ctx"), axis=0, tiled=True),
            lax.all_gather(step_proj[layer], ("fsdp", "ctx"), axis=0, tiled=True),
            lax.all_gather(mixer_out[layer], ("fsdp", "ctx"), axis=0, tiled=True),
        )
        gate_w, inner_w, state_w, step_w, mixer_w = mats
        inverse = None
        normed = rms_apply(hidden, prenorm[layer]).astype(jnp.bfloat16)
        gate = project(normed, gate_w, feat_dim)
        raw = jnp.concatenate(
            [
                project(normed, inner_w, feat_dim).astype(jnp.bfloat16),
                project(normed, state_w, feat_dim).astype(jnp.bfloat16),
            ],
            1,
        )
        step_raw = project(normed, step_w, feat_dim)
        kept_step.append(step_raw)
        before = passed_along(raw[length - (taps - 1) :], "ctx", 1)
        padded = jnp.concatenate([before, raw], 0).astype(jnp.float32)
        kernel, offset = layer_kernel(layer)
        act = conv_apply(padded, seg_padded, kernel, offset)
        inner, bmat, cmat, step = split_act(act, layer)
        decay = -jnp.exp(decay_log[layer])
        partial_mixed, produced = ssd_block(
            inner, bmat, cmat, step, decay, skip_gain[layer], seg_here, cont, zeros_state
        )
        flow = inflow(step, decay, seg_here, cont)
        incoming = prefix((flow[-1], produced), "ctx", link, identity)[1]
        mixed = partial_mixed + jnp.einsum("th,tn,hpn->thp", flow, cmat, incoming, precision=HIGH)
        mixed = mixed.reshape(length, inner_local)
        gated = mixed * jax.nn.silu(gate)
        squares = lax.psum(jnp.sum(gated * gated, 1), "tp")
        scale = lax.rsqrt(squares / inner_all + EPSILON)
        normout = (gated * scale[:, None] * norm_gain[layer]).astype(jnp.bfloat16)
        projected = lax.psum(contract_cols(normout, mixer_w), "tp")
        stored = None
        kept.append(
            (hidden, inverse, stored, normed, gate, padded, incoming, mixed, gated, scale, normout)
        )
        hidden = hidden + projected
    output = hidden
    shard_grads = [None] * layers
    small_grads = [None] * layers
    for layer in reversed(range(layers)):
        hidden_in, inverse, stored, normed, gate, padded, incoming, mixed, gated, scale, normout = (
            kept[layer]
        )
        mats = (
            lax.all_gather(gate_proj[layer], ("fsdp", "ctx"), axis=0, tiled=True),
            lax.all_gather(inner_proj[layer], ("fsdp", "ctx"), axis=0, tiled=True),
            lax.all_gather(state_proj[layer], ("fsdp", "ctx"), axis=0, tiled=True),
            lax.all_gather(step_proj[layer], ("fsdp", "ctx"), axis=0, tiled=True),
            lax.all_gather(mixer_out[layer], ("fsdp", "ctx"), axis=0, tiled=True),
        )
        gate_w, inner_w, state_w, step_w, mixer_w = mats
        gain = norm_gain[layer]
        back_b = back.astype(jnp.bfloat16)
        d_out = project(back_b, mixer_w, feat_dim)
        mixer_grad = grad_rows(back_b, normout, feat_dim)
        norm_grad = jnp.sum(d_out * gated * scale[:, None], 0)
        inner_total = lax.psum(jnp.sum(d_out * gain * gated, 1), "tp")
        d_gated = (
            scale[:, None] * gain * d_out - gated * (scale**3 * inner_total / inner_all)[:, None]
        )
        sigma = jax.nn.sigmoid(gate)
        d_mixed = d_gated * gate * sigma
        d_gate = (d_gated * mixed * sigma * (1.0 + gate * (1.0 - sigma))).astype(jnp.bfloat16)
        kernel, offset = layer_kernel(layer)
        act, conv_pull = jax.vjp(
            lambda pad, ker, off: conv_apply(pad, seg_padded, ker, off), padded, kernel, offset
        )
        inner, bmat, cmat, step = split_act(act, layer)
        decay = -jnp.exp(decay_log[layer])
        flow = inflow(step, decay, seg_here, cont)
        d_mixed3 = d_mixed.reshape(length, heads_local, head_size)
        adjoint = jnp.einsum("th,thp,tn->hpn", flow, d_mixed3, cmat, precision=HIGH)
        carried = entering((flow[-1], adjoint), "ctx", link, identity)[1]

        def mixer_local(inner_v, bmat_v, cmat_v, step_v, decay_v, skip_v, entry):
            part_v, produced_v = ssd_block(
                inner_v, bmat_v, cmat_v, step_v, decay_v, skip_v, seg_here, cont, zeros_state
            )
            flow_v = inflow(step_v, decay_v, seg_here, cont)
            result_v = part_v + jnp.einsum("th,tn,hpn->thp", flow_v, cmat_v, entry, precision=HIGH)
            return (result_v, flow_v[-1][:, None, None] * entry + produced_v)

        _, ssd_pull = jax.vjp(
            mixer_local, inner, bmat, cmat, step, decay, skip_gain[layer], incoming
        )
        g_inner, g_bmat, g_cmat, g_step, g_decay, skip_grad, _ = ssd_pull((d_mixed3, carried))
        g_state = lax.psum(jnp.concatenate([g_bmat, g_cmat], 1).astype(jnp.bfloat16), "tp").astype(
            jnp.float32
        )
        g_act = jnp.concatenate([g_inner.reshape(length, inner_local), g_state], 1)
        g_padded, kernel_grad, offset_grad = conv_pull(g_act)
        returned = passed_along(g_padded[: taps - 1], "ctx", -1)
        g_raw = g_padded[taps - 1 :] + jnp.concatenate(
            [jnp.zeros((length - (taps - 1), g_padded.shape[1]), jnp.float32), returned], 0
        )
        g_step_raw = g_step * jax.nn.sigmoid(kept_step[layer] + step_bias[layer])
        g_inner_b = g_raw[:, :inner_local].astype(jnp.bfloat16)
        g_state_b = g_raw[:, inner_local:].astype(jnp.bfloat16)
        g_step_b = g_step_raw.astype(jnp.bfloat16)
        partial_normed = (
            contract_cols(d_gate, gate_w)
            + contract_cols(g_inner_b, inner_w)
            + contract_cols(g_step_b, step_w)
        )
        d_normed = lax.psum(partial_normed.astype(jnp.bfloat16), "tp").astype(
            jnp.float32
        ) + contract_cols(g_state_b, state_w)
        _, norm_pull = jax.vjp(rms_apply, hidden_in, prenorm[layer])
        d_hidden, prenorm_full = norm_pull(d_normed)
        prenorm_grad = lax.dynamic_slice_in_dim(prenorm_full, feat_start, feat)
        shard_grads[layer] = (
            lax.psum_scatter(
                grad_rows(normed, d_gate, feat_dim),
                ("fsdp", "ctx"),
                scatter_dimension=0,
                tiled=True,
            ),
            lax.psum_scatter(
                grad_rows(normed, g_inner_b, feat_dim),
                ("fsdp", "ctx"),
                scatter_dimension=0,
                tiled=True,
            ),
            lax.psum_scatter(
                grad_rows(normed, g_state_b, feat_dim),
                ("fsdp", "ctx"),
                scatter_dimension=0,
                tiled=True,
            ),
            lax.psum_scatter(
                grad_rows(normed, g_step_b, feat_dim),
                ("fsdp", "ctx"),
                scatter_dimension=0,
                tiled=True,
            ),
            lax.psum_scatter(mixer_grad, ("fsdp", "ctx"), scatter_dimension=0, tiled=True),
        )
        back = back + d_hidden
        small_grads[layer] = (
            prenorm_grad,
            kernel_grad[:, :inner_local],
            offset_grad[:inner_local],
            kernel_grad[:, inner_local:],
            offset_grad[inner_local:],
            jnp.sum(g_step_raw, 0),
            g_decay * decay,
            skip_grad,
            norm_grad,
        )
    output = lax.dynamic_slice_in_dim(output, feat_start, feat, 1)
    back = lax.dynamic_slice_in_dim(back, feat_start, feat, 1)

    def stack_member(groups, member):
        return jnp.stack([groups[layer][member] for layer in range(layers)])

    summed = lax.psum(
        (
            stack_member(small_grads, 0),
            stack_member(small_grads, 1),
            stack_member(small_grads, 2),
            stack_member(small_grads, 3),
            stack_member(small_grads, 4),
            stack_member(small_grads, 5),
            stack_member(small_grads, 6),
            stack_member(small_grads, 7),
            stack_member(small_grads, 8),
        ),
        ("fsdp", "ctx"),
    )
    return (
        output,
        back,
        summed[0],
        stack_member(shard_grads, 0),
        stack_member(shard_grads, 1),
        stack_member(shard_grads, 2),
        stack_member(shard_grads, 3),
        summed[1],
        summed[2],
        summed[3],
        summed[4],
        summed[5],
        summed[6],
        summed[7],
        summed[8],
        stack_member(shard_grads, 4),
    )


def solution(mesh):
    placed = (
        P(("fsdp", "ctx"), None),
        P("fsdp", None),
        P(("fsdp", "ctx"), None),
        P(),
        P(None, ("fsdp", "ctx"), "tp"),
        P(None, ("fsdp", "ctx"), "tp"),
        P(None, ("fsdp", "ctx"), None),
        P(None, ("fsdp", "ctx"), "tp"),
        P(None, None, "tp"),
        P(None, "tp"),
        P(),
        P(),
        P(None, "tp"),
        P(None, "tp"),
        P(None, "tp"),
        P(None, "tp"),
        P(None, ("fsdp", "ctx"), "tp"),
    )
    return jax.shard_map(
        body,
        mesh=mesh,
        in_specs=placed,
        out_specs=(
            P(("fsdp", "ctx"), "tp"),
            P(("fsdp", "ctx"), "tp"),
            P(None, "tp"),
            P(None, ("fsdp", "ctx"), "tp"),
            P(None, ("fsdp", "ctx"), "tp"),
            P(None, ("fsdp", "ctx"), None),
            P(None, ("fsdp", "ctx"), "tp"),
            P(None, None, "tp"),
            P(None, "tp"),
            P(),
            P(),
            P(None, "tp"),
            P(None, "tp"),
            P(None, "tp"),
            P(None, "tp"),
            P(None, ("fsdp", "ctx"), "tp"),
        ),
        check_vma=False,
    )
```

profile of v0, /device:TPU:0, one launch (start us, length us, event | category | flops | bytes accessed | tf_op | source)
XLA Modules:
  0.0 1336.5 jit_solution(7054659529950893054)
XLA Ops:
  10.1 33.3 %all-gather = bf16[1,768,384]{2,1,0:T(8,128)(2,1)S(1)} all-gather(bf16[1,96,384]{2,1,0:T(8,128)(2,1)S(1)} %get-tuple-element.1111), channel_id=2, replica_groups=mesh['fsdp'=4,'ctx'=2,'tp'=4] {'fsdp','ctx'}, dimensions={1}, use_global_device_ids=true | all-gather | bytes 663552 | tf_op jit(solution)/shard_map/all_gather | solution.py:211
  43.4 31.1 %all-gather.1 = bf16[1,768,256]{2,1,0:T(8,128)(2,1)S(1)} all-gather(bf16[1,96,256]{2,1,0:T(8,128)(2,1)S(1)} %get-tuple-element.1115), channel_id=3, replica_groups=mesh['fsdp'=4,'ctx'=2,'tp'=4] {'fsdp','ctx'}, dimensions={1}, use_global_device_ids=true | all-gather | bytes 442368 | tf_op jit(solution)/shard_map/all_gather | solution.py:212
  75.6 3.7 collective-permute-start
  83.2 31.1 %all-gather.2 = bf16[1,768,6]{2,0,1:T(2,128)(2,1)S(1)} all-gather(bf16[1,96,6]{2,0,1:T(2,128)(2,1)S(1)} %copy.311), channel_id=4, replica_groups=mesh['fsdp'=4,'ctx'=2,'tp'=4] {'fsdp','ctx'}, dimensions={1}, use_global_device_ids=true | all-gather | bytes 10368 | tf_op jit(solution)/shard_map/all_gather | solution.py:213
  122.1 33.6 %all-gather.4 = bf16[1,768,384]{2,1,0:T(8,128)(2,1)} all-gather(bf16[1,96,384]{2,1,0:T(8,128)(2,1)S(1)} %get-tuple-element.1109), channel_id=6, replica_groups=mesh['fsdp'=4,'ctx'=2,'tp'=4] {'fsdp','ctx'}, dimensions={1}, use_global_device_ids=true | all-gather | bytes 663552 | tf_op jit(solution)/shard_map/all_gather | solution.py:210
  156.4 31.6 %all-gather.5 = bf16[1,768,384]{2,1,0:T(8,128)(2,1)S(1)} all-gather(bf16[1,96,384]{2,1,0:T(8,128)(2,1)S(1)} %get-tuple-element.1112), channel_id=7, replica_groups=mesh['fsdp'=4,'ctx'=2,'tp'=4] {'fsdp','ctx'}, dimensions={1}, use_global_device_ids=true | all-gather | bytes 663552 | tf_op jit(solution)/shard_map/all_gather | solution.py:214
  187.9 31.9 %all-gather.6 = bf16[1,768,384]{2,1,0:T(8,128)(2,1)S(1)} all-gather(bf16[1,96,384]{2,1,0:T(8,128)(2,1)S(1)} %get-tuple-element.1110), channel_id=8, replica_groups=mesh['fsdp'=4,'ctx'=2,'tp'=4] {'fsdp','ctx'}, dimensions={1}, use_global_device_ids=true | all-gather | bytes 663552 | tf_op jit(solution)/shard_map/all_gather | solution.py:211
  219.8 33.5 %all-gather.10 = bf16[1,768,384]{2,1,0:T(8,128)(2,1)} all-gather(bf16[1,96,384]{2,1,0:T(8,128)(2,1)S(1)} %get-tuple-element.1108), channel_id=12, replica_groups=mesh['fsdp'=4,'ctx'=2,'tp'=4] {'fsdp','ctx'}, dimensions={1}, use_global_device_ids=true | all-gather | bytes 663552 | tf_op jit(solution)/shard_map/all_gather | solution.py:210
  253.3 33.3 %all-gather.11 = bf16[1,768,384]{2,1,0:T(8,128)(2,1)} all-gather(bf16[1,96,384]{2,1,0:T(8,128)(2,1)S(1)} %get-tuple-element.1113), channel_id=13, replica_groups=mesh['fsdp'=4,'ctx'=2,'tp'=4] {'fsdp','ctx'}, dimensions={1}, use_global_device_ids=true | all-gather | bytes 663552 | tf_op jit(solution)/shard_map/all_gather | solution.py:214
  286.6 4.2 all-gather.14
  294.6 5.3 all-gather.3
  300.5 1.8 fusion.10
  302.5 2.1 multiply_reduce_fusion.35
  304.7 5.8 psum.133
  312.4 31.0 %all-gather.8 = bf16[1,768,6]{2,0,1:T(2,128)(2,1)S(1)} all-gather(bf16[1,96,6]{2,0,1:T(2,128)(2,1)S(1)} %copy.312), channel_id=10, replica_groups=mesh['fsdp'=4,'ctx'=2,'tp'=4] {'fsdp','ctx'}, dimensions={1}, use_global_device_ids=true | all-gather | bytes 10368 | tf_op jit(solution)/shard_map/all_gather | solution.py:213
  344.5 31.0 %all-gather.7 = bf16[1,768,256]{2,1,0:T(8,128)(2,1)S(1)} all-gather(bf16[1,96,256]{2,1,0:T(8,128)(2,1)S(1)} %get-tuple-element.1114), channel_id=9, replica_groups=mesh['fsdp'=4,'ctx'=2,'tp'=4] {'fsdp','ctx'}, dimensions={1}, use_global_device_ids=true | all-gather | bytes 442368 | tf_op jit(solution)/shard_map/all_gather | solution.py:212
  378.0 1.6 collective-permute-start.1
  381.4 4.2 all-gather.15
  392.4 5.4 all-gather.9
  398.9 2.7 fusion.11
  401.7 1.7 copy.225
  403.4 2.1 multiply_reduce_fusion.34
  405.5 5.6 psum.135
  411.2 2.8 multiply_reduce_fusion.18
  413.9 6.9 psum.137
  420.9 2.7 multiply_reduce_fusion.20
  423.6 1.7 copy.228
  426.6 5.4 all-gather.12
  437.2 1.6 fusion.61
  439.9 1.9 multiply_reduce_fusion.30
  448.4 2.0 multiply_add_fusion.3
  450.3 1.7 copy.234
  460.1 27.2 %all-reduce.37.cloned.1.call-done = bf16[128,256]{1,0:T(8,128)(2,1)} async-done(((bf16[128,256]{1,0:T(8,128)(2,1)}), bf16[128,256]{1,0:T(8,128)(2,1)}) %all-reduce.37.cloned.1.call-update) | async-done | bytes 65552 | tf_op jit(solution)/shard_map/psum | solution.py:302
  488.2 2.0 multiply_reduce_fusion.11
  492.0 4.1 collective-permute-done.2
  499.0 30.1 %all-reduce.39.cloned.1.call-done = bf16[128,768]{1,0:T(8,128)(2,1)} async-done(((bf16[128,768]{1,0:T(8,128)(2,1)}), bf16[128,768]{1,0:T(8,128)(2,1)}) %all-reduce.39.cloned.1.call-update) | async-done | bytes 196624 | tf_op jit(solution)/shard_map/psum | solution.py:320
  529.1 2.0 multiply_reduce_fusion
  532.3 1.5 multiply_reduce_fusion.19
  533.9 5.7 psum.140
  539.6 2.5 multiply_reduce_fusion.21
  543.9 5.3 all-gather.13
  550.2 1.6 fusion.63
  553.2 1.9 multiply_reduce_fusion.24
  556.2 1.7 multiply_add_fusion.2
  571.8 2.0 fusion.34
  573.7 20.5 %all-reduce.41.cloned.1.call-done = bf16[128,256]{1,0:T(8,128)(2,1)} async-done(((bf16[128,256]{1,0:T(8,128)(2,1)}), bf16[128,256]{1,0:T(8,128)(2,1)}) %all-reduce.41.cloned.1.call-update) | async-done | bytes 65552 | tf_op jit(solution)/shard_map/psum | solution.py:302
  598.3 4.1 collective-permute-done.3
  614.7 44.9 %reduce-scatter.33.cloned.1.call-done = f32[96,6]{1,0:T(8,128)} async-done(((f32[768,6]{1,0:T(8,128)}), f32[96,6]{1,0:T(8,128)}) %reduce-scatter.33.cloned.1.call-update) | async-done | bytes 2320
  663.3 60.6 %reduce-scatter.31.cloned.1.call-done = f32[96,6]{1,0:T(8,128)} async-done(((f32[768,6]{1,0:T(8,128)}), f32[96,6]{1,0:T(8,128)}) %reduce-scatter.31.cloned.1.call-update) | async-done | bytes 2320
  725.4 32.7 %all-reduce.35.cloned.1.call-done = f32[128,768]{1,0:T(8,128)} async-done(((f32[128,768]{1,0:T(8,128)}), f32[128,768]{1,0:T(8,128)}) %all-reduce.35.cloned.1.call-update) | async-done | bytes 393232 | tf_op jit(solution)/shard_map/psum | solution.py:246
  759.9 33.1 %all-reduce.43.cloned.1.call-done = bf16[128,768]{1,0:T(8,128)(2,1)} async-done(((bf16[128,768]{1,0:T(8,128)(2,1)}), bf16[128,768]{1,0:T(8,128)(2,1)}) %all-reduce.43.cloned.1.call-update) | async-done | bytes 196624 | tf_op jit(solution)/shard_map/psum | solution.py:320
  795.5 38.1 %all-reduce.25 = (f32[2,192]{1,0:T(2,128)}, f32[2,4,384]{2,1,0:T(4,128)}, f32[2,384]{1,0:T(2,128)}, f32[2,4,256]{2,1,0:T(4,128)}, f32[2,256]{1,0:T(2,128)}, /*in...) all-reduce(f32[2,192]{1,0:T(2,128)S(1)} %pad_maximum_fusion.19, ...), channel_id=1, replica_groups=mesh['fsdp'=4,'ctx'=2,'tp'=4] {'fsdp','ctx'}, use_global_device_ids=true, to_apply=%region_53.54 | all-reduce | flops 7588 | bytes 60704 | tf_op jit(solution)/shard_map/psum | solution.py:371
  833.6 26.1 %reduce-scatter.25.cloned.1.call-done = f32[96,256]{1,0:T(8,128)} async-done(((f32[768,256]{1,0:T(8,128)}), f32[96,256]{1,0:T(8,128)}) %reduce-scatter.25.cloned.1.call-update) | async-done | bytes 98320 | tf_op jit(solution)/shard_map/reduce_scatter | solution.py:339
  859.7 65.4 %reduce-scatter.23.cloned.1.call-done = f32[96,256]{1,0:T(8,128)} async-done(((f32[768,256]{1,0:T(8,128)}), f32[96,256]{1,0:T(8,128)}) %reduce-scatter.23.cloned.1.call-update) | async-done | bytes 98320 | tf_op jit(solution)/shard_map/reduce_scatter | solution.py:339
  925.1 1.6 pad_maximum_fusion.5
  926.8 66.0 %reduce-scatter.29.cloned.1.call-done = f32[96,384]{1,0:T(8,128)} async-done(((f32[768,384]{1,0:T(8,128)}), f32[96,384]{1,0:T(8,128)}) %reduce-scatter.29.cloned.1.call-update) | async-done | bytes 147472 | tf_op jit(solution)/shard_map/reduce_scatter | solution.py:351
  992.8 67.1 %reduce-scatter.27.cloned.1.call-done = f32[96,384]{1,0:T(8,128)} async-done(((f32[768,384]{1,0:T(8,128)}), f32[96,384]{1,0:T(8,128)}) %reduce-scatter.27.cloned.1.call-update) | async-done | bytes 147472 | tf_op jit(solution)/shard_map/reduce_scatter | solution.py:351
  1059.8 1.7 pad_maximum_fusion.4
  1061.5 65.5 %reduce-scatter.17.cloned.1.call-done = f32[96,384]{1,0:T(8,128)} async-done(((f32[768,384]{1,0:T(8,128)}), f32[96,384]{1,0:T(8,128)}) %reduce-scatter.17.cloned.1.call-update) | async-done | bytes 147472 | tf_op jit(solution)/shard_map/reduce_scatter | solution.py:327
  1127.1 67.1 %reduce-scatter.15.cloned.1.call-done = f32[96,384]{1,0:T(8,128)} async-done(((f32[768,384]{1,0:T(8,128)}), f32[96,384]{1,0:T(8,128)}) %reduce-scatter.15.cloned.1.call-update) | async-done | bytes 147472 | tf_op jit(solution)/shard_map/reduce_scatter | solution.py:327
  1194.2 1.7 pad_maximum_fusion.2
  1195.9 65.3 %reduce-scatter.21.cloned.1.call-done = f32[96,384]{1,0:T(8,128)} async-done(((f32[768,384]{1,0:T(8,128)}), f32[96,384]{1,0:T(8,128)}) %reduce-scatter.21.cloned.1.call-update) | async-done | bytes 147472 | tf_op jit(solution)/shard_map/reduce_scatter | solution.py:333
  1261.2 67.0 %reduce-scatter.19.cloned.1.call-done = f32[96,384]{1,0:T(8,128)} async-done(((f32[768,384]{1,0:T(8,128)}), f32[96,384]{1,0:T(8,128)}) %reduce-scatter.19.cloned.1.call-update) | async-done | bytes 147472 | tf_op jit(solution)/shard_map/reduce_scatter | solution.py:333
  1328.2 1.7 pad_maximum_fusion.3
  (618 shorter events, 107.4 us)
Async XLA Ops:
  7.2 67.3 %copy-start = (bf16[128,768]{1,0:T(8,128)(2,1)S(1)}, bf16[128,768]{1,0:T(8,128)(2,1)}, u32[]{:S(2)}) copy-start(bf16[128,768]{1,0:T(8,128)(2,1)} %param.25) | copy-start | bytes 589828
  7.2 36.2 %copy-start.45 = (bf16[2,96,256]{2,1,0:T(8,128)(2,1)S(1)}, bf16[2,96,256]{2,1,0:T(8,128)(2,1)}, u32[]{:S(2)}) copy-start(bf16[2,96,256]{2,1,0:T(8,128)(2,1)} %param.31) | copy-start | bytes 294916
  7.2 368.3 %all-reduce.33.cloned.1.call-start = ((), (), s32[]{:S(2)}) async-start(), calls=%async_computation.10 | async-start | bytes 786432 | tf_op jit(solution)/shard_map/psum | solution.py:246
  8.3 66.4 %copy-start.160 = (f32[128]{0:T(128)}, f32[128]{0:T(128)S(1)}, u32[]{:S(2)}) copy-start(f32[128]{0:T(128)S(1)} %multiply_reduce_fusion.7) | copy-start | bytes 1540
  8.3 106.8 %copy-start.74 = (f32[128]{0:T(128)}, f32[128]{0:T(128)S(1)}, u32[]{:S(2)}) copy-start(f32[128]{0:T(128)S(1)} %fusion.214) | copy-start | bytes 1540
  43.4 35.9 %copy-start.155 = (s32[1,256]{1,0:T(1,128)S(1)}, s32[1,256]{1,0:T(1,128)}, u32[]{:S(2)}) copy-start(s32[1,256]{1,0:T(1,128)} %param.26) | copy-start | bytes 3076
  43.4 39.1 %copy-start.108 = (bf16[2,96,6]{1,0,2:T(2,128)(2,1)S(1)}, bf16[2,96,6]{1,0,2:T(2,128)(2,1)}, u32[]{:S(2)}) copy-start(bf16[2,96,6]{1,0,2:T(2,128)(2,1)} %param.32) | copy-start | bytes 6916
  75.2 39.3 %copy-start.138 = (f32[2,6]{1,0:T(2,128)S(1)}, f32[2,6]{1,0:T(2,128)}, u32[]{:S(2)}) copy-start(f32[2,6]{1,0:T(2,128)} %param.38) | copy-start | bytes 148
  75.2 39.3 %copy-start.157 = (f32[2,6]{1,0:T(2,128)S(1)}, f32[2,6]{1,0:T(2,128)}, u32[]{:S(2)}) copy-start(f32[2,6]{1,0:T(2,128)} %param.37) | copy-start | bytes 148
  75.5 43.0 %copy-start.107 = (f32[2,4,384]{2,1,0:T(4,128)S(1)}, f32[2,4,384]{2,1,0:T(4,128)}, u32[]{:S(2)}) copy-start(f32[2,4,384]{2,1,0:T(4,128)} %param.33) | copy-start | bytes 36868
  75.5 43.6 %copy-start.120 = (f32[2,4,256]{2,1,0:T(4,128)S(1)}, f32[2,4,256]{2,1,0:T(4,128)}, u32[]{:S(2)}) copy-start(f32[2,4,256]{2,1,0:T(4,128)} %param.35) | copy-start | bytes 24580
  75.5 44.2 %copy-start.140 = (f32[2,384]{1,0:T(2,128)S(1)}, f32[2,384]{1,0:T(2,128)}, u32[]{:S(2)}) copy-start(f32[2,384]{1,0:T(2,128)} %param.34) | copy-start | bytes 9220
  75.5 44.8 %copy-start.142 = (f32[2,256]{1,0:T(2,128)S(1)}, f32[2,256]{1,0:T(2,128)}, u32[]{:S(2)}) copy-start(f32[2,256]{1,0:T(2,128)} %param.36) | copy-start | bytes 6148
  75.5 46.0 %copy-start.156 = (f32[2,6]{1,0:T(2,128)S(1)}, f32[2,6]{1,0:T(2,128)}, u32[]{:S(2)}) copy-start(f32[2,6]{1,0:T(2,128)} %param.39) | copy-start | bytes 148
  75.5 46.6 %copy-start.43 = (bf16[2,96,384]{2,1,0:T(8,128)(2,1)S(1)}, bf16[2,96,384]{2,1,0:T(8,128)(2,1)}, u32[]{:S(2)}) copy-start(bf16[2,96,384]{2,1,0:T(8,128)(2,1)} %param.29) | copy-start | bytes 442372
  75.6 216.2 %collective-permute-start = (bf16[3,640]{1,0:T(4,128)(2,1)S(1)}, bf16[3,640]{1,0:T(4,128)(2,1)S(1)}, u32[]{:S(2)}, u32[]{:S(2)}) collective-permute-start(bf16[3,640]{1,0:T(4,128)(2,1)S(1)} %pad_maximum_fusion.12), channel_id=1, source_target_pairs={{0,4},{1,5},{2,6},{3,7},{8,12},{9,13},{10,14},{11,15},{16,20},{17,... | collective-permute-start | bytes 11528 | tf_op jit(solution)/shard_map/ppermute | solution.py:16
  82.5 73.3 %copy-start.103 = (f32[128]{0:T(128)}, f32[128]{0:T(128)S(1)}, u32[]{:S(2)}) copy-start(f32[128]{0:T(128)S(1)} %convert_reduce_fusion) | copy-start | bytes 1540
  114.3 41.5 %copy-start.141 = (f32[2,384]{1,0:T(2,128)S(1)}, f32[2,384]{1,0:T(2,128)}, u32[]{:S(2)}) copy-start(f32[2,384]{1,0:T(2,128)} %param.40) | copy-start | bytes 9220
  114.3 42.1 %copy-start.44 = (bf16[2,96,384]{2,1,0:T(8,128)(2,1)S(1)}, bf16[2,96,384]{2,1,0:T(8,128)(2,1)}, u32[]{:S(2)}) copy-start(bf16[2,96,384]{2,1,0:T(8,128)(2,1)} %param.41) | copy-start | bytes 442372
  114.6 73.4 %copy-start.55 = (bf16[1,768,6]{1,2,0:T(8,128)(2,1)}, bf16[1,768,6]{1,2,0:T(8,128)(2,1)S(1)}, u32[]{:S(2)}) copy-start(bf16[1,768,6]{1,2,0:T(8,128)(2,1)S(1)} %copy.209) | copy-start | bytes 27652
  115.2 72.8 %copy-start.148 = (f32[6]{0:T(128)}, f32[6]{0:T(128)S(1)}, u32[]{:S(2)}) copy-start(f32[6]{0:T(128)S(1)} %get-tuple-element.1168) | copy-start | bytes 76
  116.0 178.2 %copy-start.90 = (f32[128,6]{0,1:T(8,128)}, f32[128,6]{0,1:T(8,128)S(1)}, u32[]{:S(2)}) copy-start(f32[128,6]{0,1:T(8,128)S(1)} %get-tuple-element.1136) | copy-start | bytes 9220
  116.3 174.6 %copy-start.23 = (f32[128,6]{1,0:T(8,128)}, f32[128,6]{1,0:T(8,128)S(1)}, u32[]{:S(2)}) copy-start(f32[128,6]{1,0:T(8,128)S(1)} %reduce_window_sum.90) | copy-start | bytes 9220
  117.7 174.1 %copy-start.76 = (f32[128]{0:T(128)}, f32[128]{0:T(128)S(1)}, u32[]{:S(2)}) copy-start(f32[128]{0:T(128)S(1)} %get-tuple-element.1146) | copy-start | bytes 1540
  117.7 174.1 %copy-start.80 = (f32[128]{0:T(128)}, f32[128]{0:T(128)S(1)}, u32[]{:S(2)}) copy-start(f32[128]{0:T(128)S(1)} %get-tuple-element.1147) | copy-start | bytes 1540
  117.7 174.1 %copy-start.84 = (f32[128]{0:T(128)}, f32[128]{0:T(128)S(1)}, u32[]{:S(2)}) copy-start(f32[128]{0:T(128)S(1)} %get-tuple-element.1148) | copy-start | bytes 1540
  187.9 123.1 %copy-start.2 = (bf16[1,768,384]{2,1,0:T(8,128)(2,1)}, bf16[1,768,384]{2,1,0:T(8,128)(2,1)S(1)}, u32[]{:S(2)}) copy-start(bf16[1,768,384]{2,1,0:T(8,128)(2,1)S(1)} %all-gather.5) | copy-start | bytes 1769476
  304.7 39.0 %copy-start.11 = (f32[128,384]{1,0:T(8,128)}, f32[128,384]{1,0:T(8,128)S(1)}, u32[]{:S(2)}) copy-start(f32[128,384]{1,0:T(8,128)S(1)} %get-tuple-element.1089) | copy-start | bytes 589828
  311.0 33.4 %copy-start.88 = (f32[4,384]{1,0:T(4,128)S(1)}, f32[4,384]{1,0:T(4,128)}, u32[]{:S(2)}) copy-start(f32[4,384]{1,0:T(4,128)} %get-tuple-element.1130) | copy-start | bytes 18436
  311.0 33.4 %copy-start.98 = (f32[4,256]{1,0:T(4,128)S(1)}, f32[4,256]{1,0:T(4,128)}, u32[]{:S(2)}) copy-start(f32[4,256]{1,0:T(4,128)} %get-tuple-element.1132) | copy-start | bytes 12292
  312.2 175.1 %all-reduce.37.cloned.1.call-start = ((), (), s32[]{:S(2)}) async-start(), calls=%async_computation.12 | async-start | bytes 131072 | tf_op jit(solution)/shard_map/psum | solution.py:302
  343.7 36.0 %copy-start.57 = (bf16[1,768,6]{1,2,0:T(8,128)(2,1)}, bf16[1,768,6]{1,2,0:T(8,128)(2,1)S(1)}, u32[]{:S(2)}) copy-start(bf16[1,768,6]{1,2,0:T(8,128)(2,1)S(1)} %copy.219) | copy-start | bytes 27652
  344.4 43.5 %copy-start.66 = (f32[640]{0:T(1024)}, f32[640]{0:T(1024)S(1)}, u32[]{:S(2)}) copy-start(f32[640]{0:T(1024)S(1)} %get-tuple-element.1004) | copy-start | bytes 7684
  344.5 43.5 %copy-start.68 = (f32[640]{0:T(1024)}, f32[640]{0:T(1024)S(1)}, u32[]{:S(2)}) copy-start(f32[640]{0:T(1024)S(1)} %get-tuple-element.1005) | copy-start | bytes 7684
  344.5 43.5 %copy-start.70 = (f32[640]{0:T(1024)}, f32[640]{0:T(1024)S(1)}, u32[]{:S(2)}) copy-start(f32[640]{0:T(1024)S(1)} %get-tuple-element.1006) | copy-start | bytes 7684
  344.5 43.5 %copy-start.72 = (f32[640]{0:T(1024)}, f32[640]{0:T(1024)S(1)}, u32[]{:S(2)}) copy-start(f32[640]{0:T(1024)S(1)} %get-tuple-element.1007) | copy-start | bytes 7684
  378.0 9.9 collective-permute-start.1
  389.0 36.3 %copy-start.6 = (f32[128,640]{1,0:T(8,128)}, f32[128,640]{1,0:T(8,128)S(1)}, u32[]{:S(2)}) copy-start(f32[128,640]{1,0:T(8,128)S(1)} %get-tuple-element.1084) | copy-start | bytes 983044
  456.5 72.6 %all-reduce.39.cloned.1.call-start = ((), (), s32[]{:S(2)}) async-start(), calls=%async_computation.13 | async-start | bytes 393216 | tf_op jit(solution)/shard_map/psum | solution.py:320
  490.4 5.7 collective-permute-start.2
  497.9 96.4 %all-reduce.41.cloned.1.call-start = ((), (), s32[]{:S(2)}) async-start(), calls=%async_computation.14 | async-start | bytes 131072 | tf_op jit(solution)/shard_map/psum | solution.py:302
  499.0 33.3 %copy-start.111 = (f32[128]{0:T(128)S(1)}, f32[128]{0:T(128)}, u32[]{:S(2)}) copy-start(f32[128]{0:T(128)} %copy-done.110) | copy-start | bytes 1540
  562.5 97.1 %reduce-scatter.33.cloned.1.call-start = ((), (), s32[]{:S(2)}) async-start(), calls=%async_computation.25 | async-start | bytes 442368
  563.6 160.3 %reduce-scatter.31.cloned.1.call-start = ((), (), s32[]{:S(2)}) async-start(), calls=%async_computation.24 | async-start | bytes 442368
  570.2 187.9 %all-reduce.35.cloned.1.call-start = ((), (), s32[]{:S(2)}) async-start(), calls=%async_computation.11 | async-start | bytes 786432 | tf_op jit(solution)/shard_map/psum | solution.py:246
  571.4 221.7 %all-reduce.43.cloned.1.call-start = ((), (), s32[]{:S(2)}) async-start(), calls=%async_computation.15 | async-start | bytes 393216 | tf_op jit(solution)/shard_map/psum | solution.py:320
  596.8 5.7 collective-permute-start.3
  603.5 256.2 %reduce-scatter.25.cloned.1.call-start = ((), (), s32[]{:S(2)}) async-start(), calls=%async_computation.21 | async-start | bytes 884736 | tf_op jit(solution)/shard_map/reduce_scatter | solution.py:339
  604.8 320.3 %reduce-scatter.23.cloned.1.call-start = ((), (), s32[]{:S(2)}) async-start(), calls=%async_computation.20 | async-start | bytes 884736 | tf_op jit(solution)/shard_map/reduce_scatter | solution.py:339
  606.2 386.6 %reduce-scatter.29.cloned.1.call-start = ((), (), s32[]{:S(2)}) async-start(), calls=%async_computation.23 | async-start | bytes 1327104 | tf_op jit(solution)/shard_map/reduce_scatter | solution.py:351
  607.7 452.1 %reduce-scatter.27.cloned.1.call-start = ((), (), s32[]{:S(2)}) async-start(), calls=%async_computation.22 | async-start | bytes 1327104 | tf_op jit(solution)/shard_map/reduce_scatter | solution.py:351
  609.2 517.8 %reduce-scatter.17.cloned.1.call-start = ((), (), s32[]{:S(2)}) async-start(), calls=%async_computation.17 | async-start | bytes 1327104 | tf_op jit(solution)/shard_map/reduce_scatter | solution.py:327
  610.7 583.4 %reduce-scatter.15.cloned.1.call-start = ((), (), s32[]{:S(2)}) async-start(), calls=%async_computation.16 | async-start | bytes 1327104 | tf_op jit(solution)/shard_map/reduce_scatter | solution.py:327
  612.2 649.0 %reduce-scatter.21.cloned.1.call-start = ((), (), s32[]{:S(2)}) async-start(), calls=%async_computation.19 | async-start | bytes 1327104 | tf_op jit(solution)/shard_map/reduce_scatter | solution.py:333
  613.7 46.8 %copy-start.118 = (f32[384]{0:T(512)S(1)}, f32[384]{0:T(512)}, u32[]{:S(2)}) copy-start(f32[384]{0:T(512)} %get-tuple-element.984) | copy-start | bytes 4612
  613.7 46.8 %copy-start.116 = (f32[384]{0:T(512)S(1)}, f32[384]{0:T(512)}, u32[]{:S(2)}) copy-start(f32[384]{0:T(512)} %get-tuple-element.1071) | copy-start | bytes 4612
  613.7 47.7 %copy-start.139 = (f32[2,6]{1,0:T(2,128)S(1)}, f32[2,6]{1,0:T(2,128)}, u32[]{:S(2)}) copy-start(f32[2,6]{1,0:T(2,128)} %param.38) | copy-start | bytes 148
  613.7 47.7 %copy-start.150 = (f32[6]{0:T(128)S(1)}, f32[6]{0:T(128)}, u32[]{:S(2)}) copy-start(f32[6]{0:T(128)} %get-tuple-element.1016) | copy-start | bytes 76
  613.7 47.7 %copy-start.151 = (f32[6]{0:T(128)S(1)}, f32[6]{0:T(128)}, u32[]{:S(2)}) copy-start(f32[6]{0:T(128)} %get-tuple-element.1017) | copy-start | bytes 76
  613.7 47.7 %copy-start.153 = (f32[6]{0:T(128)S(1)}, f32[6]{0:T(128)}, u32[]{:S(2)}) copy-start(f32[6]{0:T(128)} %get-tuple-element.1014) | copy-start | bytes 76
  613.8 47.7 %copy-start.154 = (f32[6]{0:T(128)S(1)}, f32[6]{0:T(128)}, u32[]{:S(2)}) copy-start(f32[6]{0:T(128)} %get-tuple-element.1015) | copy-start | bytes 76
  613.8 714.4 %reduce-scatter.19.cloned.1.call-start = ((), (), s32[]{:S(2)}) async-start(), calls=%async_computation.18 | async-start | bytes 1327104 | tf_op jit(solution)/shard_map/reduce_scatter | solution.py:333
  663.0 130.1 %copy-start.26 = (bf16[1,768,256]{2,1,0:T(8,128)(2,1)S(1)}, bf16[1,768,256]{2,1,0:T(8,128)(2,1)}, u32[]{:S(2)}) copy-start(bf16[1,768,256]{2,1,0:T(8,128)(2,1)} %copy-done.25) | copy-start | bytes 1179652
  663.0 131.5 %copy-start.161 = (f32[128]{0:T(128)S(1)}, f32[128]{0:T(128)}, u32[]{:S(2)}) copy-start(f32[128]{0:T(128)} %copy-done.160) | copy-start | bytes 1540
  (126 other events, 753.0 us)
Sparse Core Ops, SparseCore 0:
  312.3 31.5 all-reduce.32
  456.6 30.6 all-reduce.36
  498.0 31.0 all-reduce.38
  562.6 31.6 all-reduce.40
  597.4 62.1 reduce-scatter.32
  662.7 61.1 reduce-scatter.30
  726.2 31.8 all-reduce.34
  761.0 32.0 all-reduce.42
  796.4 63.3 reduce-scatter.24
  862.9 62.1 reduce-scatter.22
  928.5 64.1 reduce-scatter.28
  996.0 63.7 reduce-scatter.26
  1063.2 63.8 reduce-scatter.16
  1130.3 63.7 reduce-scatter.14
  1197.4 63.7 reduce-scatter.20
  1264.5 63.7 reduce-scatter.18
where the time goes:
time: 1340 us
  waiting for transfers between devices  747 us (56%)
  blocking collectives  413 us (31%)
  matrix products  65.4 us (5%)
  other arithmetic  47.7 us (4%)
  local copies, waits for them, and re-layouts  36.1 us (3%)
  between operations  17.7 us (1%)
    reduce_scatter x2, waiting for transfers between devices, body(): lax.psum_scatter(mixer_grad, ('fsdp', 'ctx'), scatter_dimension=0, tiled=...  133 us
    reduce_scatter x2, waiting for transfers between devices, body(): lax.psum_scatter(grad_rows(normed, d_gate, feat_dim), ('fsdp', 'ctx'), sc...  133 us
    reduce_scatter x2, waiting for transfers between devices, body(): lax.psum_scatter(grad_rows(normed, g_inner_b, feat_dim), ('fsdp', 'ctx'),...  132 us
    unnamed x18, waiting for transfers between devices  106 us
    reduce_scatter x2, waiting for transfers between devices, body(): lax.psum_scatter(grad_rows(normed, g_state_b, feat_dim), ('fsdp', 'ctx'),...  91.5 us
    all_gather x2, blocking collectives, body(): lax.all_gather(gate_proj[layer], ('fsdp', 'ctx'), axis=0, tiled=True)  67.1 us
    all_gather x2, blocking collectives, body(): lax.all_gather(inner_proj[layer], ('fsdp', 'ctx'), axis=0, tiled=True)  65.1 us
    all_gather x2, blocking collectives, body(): lax.all_gather(mixer_out[layer], ('fsdp', 'ctx'), axis=0, tiled=True)  64.8 us
  transfers between devices with their start and end apart: 20, of which 17 were waited for; matrix products, arithmetic and copies ran while one was open for 4% of the time, Pallas kernels for 0%

commit v1 on v0

--- a/solution.py
+++ b/solution.py
@@ -1,6 +1,10 @@
+import functools
+
 import jax
 import jax.numpy as jnp
 from jax import lax
+from jax.experimental import pallas as pl
+from jax.experimental.pallas import tpu as pltpu
 from jax.sharding import PartitionSpec as P
 
 SPAN = 128
@@ -148,6 +152,307 @@
     return lax.dot_general(
         normed, delta, (((1 - feat_dim,), (0,)), ((), ())), preferred_element_type=jnp.float32
     )
+
+
+MESH = pl.DeviceIdType.MESH
+VM = pl.BlockSpec(memory_space=pltpu.VMEM)
+
+
+def remote(src, dst, send, recv, where):
+    return pltpu.make_async_remote_copy(
+        src_ref=src, dst_ref=dst, send_sem=send, recv_sem=recv, device_id=where, device_id_type=MESH
+    )
+
+
+def greet(peers):
+    barrier = pltpu.get_barrier_semaphore()
+    for peer in peers:
+        pl.semaphore_signal(barrier, inc=1, device_id=peer, device_id_type=MESH)
+    pl.semaphore_wait(barrier, len(peers))
+
+
+def weights_kernel(nz, ny, *refs):
+    shards, (win, wmix), (own_sem, zsend, zrecv, ysend, yrecv) = refs[:4], refs[4:6], refs[6:]
+    z, y = lax.axis_index("fsdp"), lax.axis_index("ctx")
+    rows, cols = shards[0].shape[1:]
+    z_at = lambda d: lax.rem(z + d, nz)
+    y_at = lambda e: lax.rem(y + e, ny)
+    greet([{"fsdp": z_at(d)} for d in range(1, nz)] + [{"ctx": y_at(e)} for e in range(1, ny)])
+
+    def region(piece, zs, ys):
+        at = pl.ds(pl.multiple_of((zs * ny + ys) * rows, rows), rows)
+        if piece == 3:
+            return wmix.at[:, at, :]
+        return win.at[:, at, pl.ds(piece * cols, cols)]
+
+    own, sends = [], []
+    for piece in range(4):
+        copy = pltpu.make_async_copy(shards[piece], region(piece, z, y), own_sem.at[piece])
+        copy.start()
+        own.append(copy)
+    zcopies, ycopies = {}, {}
+    for piece in range(4):
+        for d in range(1, nz):
+            copy = remote(
+                shards[piece],
+                region(piece, z, y),
+                zsend.at[piece, d - 1],
+                zrecv.at[piece, d - 1],
+                {"fsdp": z_at(d)},
+            )
+            copy.start()
+            zcopies[piece, d] = copy
+        for e in range(1, ny):
+            copy = remote(
+                shards[piece],
+                region(piece, z, y),
+                ysend.at[piece, 0, e - 1],
+                yrecv.at[piece, 0, e - 1],
+                {"ctx": y_at(e)},
+            )
+            copy.start()
+            ycopies[piece, 0, e] = copy
+    for piece in range(4):
+        for d in range(1, nz):
+            zcopies[piece, d].wait_recv()
+            block = region(piece, z_at(nz - d), y)
+            for e in range(1, ny):
+                copy = remote(
+                    block,
+                    block,
+                    ysend.at[piece, d, e - 1],
+                    yrecv.at[piece, d, e - 1],
+                    {"ctx": y_at(e)},
+                )
+                copy.start()
+                ycopies[piece, d, e] = copy
+    for copy in own:
+        copy.wait()
+    for copy in zcopies.values():
+        copy.wait_send()
+    for copy in ycopies.values():
+        copy.wait()
+
+
+def gather_weights(gate, inner, extra, mixer):
+    nz, ny = lax.axis_size("fsdp"), lax.axis_size("ctx")
+    layers, rows, cols = gate.shape
+    full = rows * nz * ny
+    dma = pltpu.SemaphoreType.DMA
+    return pl.pallas_call(
+        functools.partial(weights_kernel, nz, ny),
+        out_shape=(
+            jax.ShapeDtypeStruct((layers, full, 3 * cols), gate.dtype),
+            jax.ShapeDtypeStruct((layers, full, cols), gate.dtype),
+        ),
+        in_specs=[VM] * 4,
+        out_specs=(VM, VM),
+        scratch_shapes=[
+            dma((4,)),
+            dma((4, nz - 1)),
+            dma((4, nz - 1)),
+            dma((4, nz, ny - 1)),
+            dma((4, nz, ny - 1)),
+        ],
+        compiler_params=pltpu.CompilerParams(collective_id=1, has_side_effects=True),
+        name="weights",
+    )(gate, inner, extra, mixer)
+
+
+def grads_kernel(nz, layers, *refs):
+    ins = refs[: 2 * layers]
+    small = refs[2 * layers]
+    outs = refs[2 * layers + 1 : 2 * layers + 5]
+    small_out = refs[2 * layers + 5]
+    rest = refs[2 * layers + 6 :]
+    yin, ymix, pin, pmix, zin, zmix, srecv = rest[:7]
+    ysend, yrecv, zsend, zrecv, ssend, srec, sown = rest[7:]
+    ny = 2
+    z, y = lax.axis_index("fsdp"), lax.axis_index("ctx")
+    other = 1 - y
+    rows, cols = outs[0].shape[1:]
+    z_at = lambda d: lax.rem(z + d, nz)
+    peers = []
+    for d in range(nz):
+        for where in (y, other):
+            if not (d == 0 and where is y):
+                peers.append({"fsdp": z_at(d), "ctx": where})
+    greet(peers)
+    me = z * ny + y
+    keep = pltpu.make_async_copy(small, srecv.at[me], sown)
+    keep.start()
+
+    def chunk(zd, yd):
+        return pl.ds(pl.multiple_of((zd * ny + yd) * rows, rows), rows)
+
+    order = [(layer, d) for layer in range(layers) for d in list(range(1, nz)) + [0]]
+    ycopies, zcopies, scopies = {}, {}, []
+    for layer, d in order:
+        at = chunk(z_at(d), other)
+        for which, buffer in enumerate((yin, ymix)):
+            copy = remote(
+                ins[2 * layer + which].at[at, :],
+                buffer.at[layer, d],
+                ysend.at[layer, d, which],
+                yrecv.at[layer, d, which],
+                {"ctx": other},
+            )
+            copy.start()
+            ycopies[layer, d, which] = copy
+    for i, peer in enumerate(peers):
+        copy = remote(small, srecv.at[me], ssend.at[i], srec.at[i], peer)
+        copy.start()
+        scopies.append(copy)
+    for layer, d in order:
+        at = chunk(z_at(d), y)
+        for which, (got, put, land) in enumerate(((yin, pin, zin), (ymix, pmix, zmix))):
+            ycopies[layer, d, which].wait_recv()
+            total = ins[2 * layer + which][at, :].astype(jnp.float32) + got[layer, d].astype(
+                jnp.float32
+            )
+            if d:
+                put[layer, d - 1] = total.astype(jnp.bfloat16)
+                copy = remote(
+                    put.at[layer, d - 1],
+                    land.at[layer, d - 1],
+                    zsend.at[layer, d - 1, which],
+                    zrecv.at[layer, d - 1, which],
+                    {"fsdp": z_at(d)},
+                )
+                copy.start()
+                zcopies[layer, d, which] = copy
+            elif which:
+                outs[3][layer] = total
+            else:
+                for part in range(3):
+                    outs[part][layer] = total[:, part * cols : (part + 1) * cols]
+    for layer in range(layers):
+        for d in range(1, nz):
+            zcopies[layer, d, 0].wait_recv()
+            zcopies[layer, d, 1].wait_recv()
+        for part in range(3):
+            total = outs[part][layer]
+            for d in range(1, nz):
+                total = total + zin[layer, d - 1, :, part * cols : (part + 1) * cols].astype(
+                    jnp.float32
+                )
+            outs[part][layer] = total
+        total = outs[3][layer]
+        for d in range(1, nz):
+            total = total + zmix[layer, d - 1].astype(jnp.float32)
+        outs[3][layer] = total
+    keep.wait()
+    for copy in scopies:
+        copy.wait_recv()
+    total = srecv[0]
+    for i in range(1, nz * ny):
+        total = total + srecv[i]
+    small_out[...] = total
+    for copy in list(ycopies.values()) + list(zcopies.values()) + scopies:
+        copy.wait_send()
+
+
+def reduce_grads(grads, small):
+    nz = lax.axis_size("fsdp")
+    layers = len(grads) // 2
+    full, cols = grads[1].shape
+    rows = full // (2 * nz)
+    dma, bf = pltpu.SemaphoreType.DMA, jnp.bfloat16
+    return pl.pallas_call(
+        functools.partial(grads_kernel, nz, layers),
+        out_shape=tuple(jax.ShapeDtypeStruct((layers, rows, cols), jnp.float32) for _ in range(4))
+        + (jax.ShapeDtypeStruct(small.shape, jnp.float32),),
+        in_specs=[VM] * (2 * layers + 1),
+        out_specs=(VM,) * 5,
+        scratch_shapes=[
+            pltpu.VMEM((layers, nz, rows, 3 * cols), bf),
+            pltpu.VMEM((layers, nz, rows, cols), bf),
+            pltpu.VMEM((layers, nz - 1, rows, 3 * cols), bf),
+            pltpu.VMEM((layers, nz - 1, rows, cols), bf),
+            pltpu.VMEM((layers, nz - 1, rows, 3 * cols), bf),
+            pltpu.VMEM((layers, nz - 1, rows, cols), bf),
+            pltpu.VMEM((2 * nz,) + small.shape, jnp.float32),
+            dma((layers, nz, 2)),
+            dma((layers, nz, 2)),
+            dma((layers, nz - 1, 2)),
+            dma((layers, nz - 1, 2)),
+            dma((2 * nz - 1,)),
+            dma((2 * nz - 1,)),
+            dma,
+        ],
+        compiler_params=pltpu.CompilerParams(collective_id=2, has_side_effects=True),
+        name="grads",
+    )(*grads, small)
+
+
+def sum_kernel(n, tallied, *refs):
+    if tallied:
+        x, tally, out, tally_out, got, put, seen = refs[:7]
+        send, recv, send2, recv2, tsend, trecv, town = refs[7:]
+    else:
+        x, out, got, put, send, recv, send2, recv2 = refs
+    me = lax.axis_index("tp")
+    rows = x.shape[0] // n
+    at = lambda i: pl.ds(pl.multiple_of(i * rows, rows), rows)
+    peers = [lax.rem(me + d, n) for d in range(1, n)]
+    greet([{"tp": peer} for peer in peers])
+    first, second, tallies = [], [], []
+    for d, peer in enumerate(peers):
+        copy = remote(x.at[at(peer), :], got.at[d], send.at[d], recv.at[d], {"tp": peer})
+        copy.start()
+        first.append(copy)
+    if tallied:
+        keep = pltpu.make_async_copy(tally, seen.at[me], town)
+        keep.start()
+        for d, peer in enumerate(peers):
+            copy = remote(tally, seen.at[me], tsend.at[d], trecv.at[d], {"tp": peer})
+            copy.start()
+            tallies.append(copy)
+    total = x[at(me), :].astype(jnp.float32)
+    for d in range(n - 1):
+        first[d].wait_recv()
+        total = total + got[d].astype(jnp.float32)
+    put[...] = total.astype(put.dtype)
+    for d, peer in enumerate(peers):
+        copy = remote(put, out.at[at(me), :], send2.at[d], recv2.at[d], {"tp": peer})
+        copy.start()
+        second.append(copy)
+    out[at(me), :] = total.astype(put.dtype)
+    if tallied:
+        keep.wait()
+        for copy in tallies:
+            copy.wait_recv()
+        total = seen[0]
+        for i in range(1, n):
+            total = total + seen[i]
+        tally_out[...] = total
+    for copy in second:
+        copy.wait_recv()
+    for copy in first + second + tallies:
+        copy.wait_send()
+
+
+def tp_sum(x, ident, tally=None):
+    n = lax.axis_size("tp")
+    rows, cols = x.shape
+    dma = pltpu.SemaphoreType.DMA
+    tallied = tally is not None
+    block = pltpu.VMEM((n - 1, rows // n, cols), x.dtype)
+    scratch = [block, pltpu.VMEM((rows // n, cols), x.dtype)]
+    shape = jax.ShapeDtypeStruct(x.shape, x.dtype)
+    if tallied:
+        scratch.append(pltpu.VMEM((n,) + tally.shape, jnp.float32))
+        shape = (shape, jax.ShapeDtypeStruct(tally.shape, jnp.float32))
+    scratch += [dma((n - 1,))] * (6 if tallied else 4) + ([dma] if tallied else [])
+    return pl.pallas_call(
+        functools.partial(sum_kernel, n, tallied),
+        out_shape=shape,
+        in_specs=[VM] * (2 if tallied else 1),
+        out_specs=(VM, VM) if tallied else VM,
+        scratch_shapes=scratch,
+        compiler_params=pltpu.CompilerParams(collective_id=ident, has_side_effects=True),
+        name="tpsum",
+    )(*((x, tally) if tallied else (x,)))
 
 
 def body(
@@ -402,6 +707,224 @@
     )
 
 
+def body_kernels(
+    tokens,
+    segments,
+    cotangent,
+    prenorm,
+    gate_proj,
+    inner_proj,
+    state_proj,
+    step_proj,
+    inner_kernel,
+    inner_offset,
+    state_kernel,
+    state_offset,
+    step_bias,
+    decay_log,
+    skip_gain,
+    norm_gain,
+    mixer_out,
+):
+    length = tokens.shape[0]
+    model = tokens.shape[1]
+    layers = gate_proj.shape[0]
+    taps = inner_kernel.shape[1]
+    inner_local = gate_proj.shape[2]
+    heads_local = step_proj.shape[2]
+    head_size = inner_local // heads_local
+    state_size = state_proj.shape[2] // 2
+    inner_all = inner_local * lax.axis_size("tp")
+    feat = model // lax.axis_size("tp")
+    feat_start = lax.axis_index("tp") * feat
+    start = lax.axis_index("ctx") * length
+    seg_pad = jnp.concatenate([jnp.full((taps - 1,), -1, jnp.int32), segments[0]])
+    seg_padded = lax.dynamic_slice_in_dim(seg_pad, start, length + taps - 1)
+    seg_here = seg_padded[taps - 1 :]
+    cont = (seg_padded[taps - 2] == seg_padded[taps - 1]).astype(jnp.float32)
+    zeros_state = jnp.zeros((heads_local, head_size, state_size), jnp.float32)
+    identity = (jnp.ones((heads_local,), jnp.float32), zeros_state)
+
+    def layer_kernel(layer):
+        kernel = jnp.concatenate([inner_kernel[layer], state_kernel[layer]], 1)
+        offset = jnp.concatenate([inner_offset[layer], state_offset[layer]])
+        return (kernel, offset)
+
+    def split_act(act, layer):
+        inner = act[:, :inner_local].reshape(length, heads_local, head_size)
+        bmat = act[:, inner_local : inner_local + state_size]
+        cmat = act[:, inner_local + state_size :]
+        step = jax.nn.softplus(kept_step[layer] + step_bias[layer])
+        return (inner, bmat, cmat, step)
+
+    feat_dim = 1
+    hidden = tokens.astype(jnp.float32)
+    back = cotangent
+    kept = []
+    kept_step = []
+    cols = inner_local
+    pad = cols - 2 * state_size - heads_local
+    extra = jnp.concatenate(
+        [state_proj, step_proj, jnp.zeros(step_proj.shape[:2] + (pad,), step_proj.dtype)], 2
+    )
+    win, wmix = gather_weights(gate_proj, inner_proj, extra, mixer_out)
+    bf = jnp.bfloat16
+    lead = (lax.axis_index("tp") == 0).astype(bf)
+    for layer in range(layers):
+        inverse = None
+        normed = rms_apply(hidden, prenorm[layer]).astype(jnp.bfloat16)
+        wide = project(normed, win[layer], feat_dim)
+        gate = wide[:, :cols]
+        raw = wide[:, cols : 2 * cols + 2 * state_size].astype(bf)
+        step_raw = wide[:, 2 * cols + 2 * state_size :][:, :heads_local]
+        kept_step.append(step_raw)
+        before = passed_along(raw[length - (taps - 1) :], "ctx", 1)
+        padded = jnp.concatenate([before, raw], 0).astype(jnp.float32)
+        kernel, offset = layer_kernel(layer)
+        act = conv_apply(padded, seg_padded, kernel, offset)
+        inner, bmat, cmat, step = split_act(act, layer)
+        decay = -jnp.exp(decay_log[layer])
+        partial_mixed, produced = ssd_block(
+            inner, bmat, cmat, step, decay, skip_gain[layer], seg_here, cont, zeros_state
+        )
+        flow = inflow(step, decay, seg_here, cont)
+        incoming = passed_along(produced.astype(bf), "ctx", 1).astype(jnp.float32)
+        mixed = partial_mixed + jnp.einsum("th,tn,hpn->thp", flow, cmat, incoming, precision=HIGH)
+        mixed = mixed.reshape(length, inner_local)
+        gated = mixed * jax.nn.silu(gate)
+        squares = jnp.broadcast_to(jnp.sum(gated * gated, 1)[None], (8, length))
+        lifted = (gated * norm_gain[layer]).astype(bf)
+        projected, squares = tp_sum(contract_cols(lifted, wmix[layer]).astype(bf), 3, squares)
+        projected = projected.astype(jnp.float32)
+        scale = lax.rsqrt(squares[0] / inner_all + EPSILON)
+        normout = (gated * scale[:, None] * norm_gain[layer]).astype(bf)
+        stored = projected
+        kept.append(
+            (hidden, inverse, stored, normed, gate, padded, incoming, mixed, gated, scale, normout)
+        )
+        hidden = hidden + projected * scale[:, None]
+    output = hidden
+    shard_grads = [None] * layers
+    small_grads = [None] * layers
+    for layer in reversed(range(layers)):
+        hidden_in, inverse, stored, normed, gate, padded, incoming, mixed, gated, scale, normout = (
+            kept[layer]
+        )
+        gain = norm_gain[layer]
+        back_b = back.astype(jnp.bfloat16)
+        d_out = project(back_b, wmix[layer], feat_dim)
+        mixer_grad = grad_rows(back_b, normout, feat_dim)
+        norm_grad = jnp.sum(d_out * gated * scale[:, None], 0)
+        inner_total = jnp.sum(back_b.astype(jnp.float32) * stored, 1)
+        d_gated = (
+            scale[:, None] * gain * d_out - gated * (scale**3 * inner_total / inner_all)[:, None]
+        )
+        sigma = jax.nn.sigmoid(gate)
+        d_mixed = d_gated * gate * sigma
+        d_gate = (d_gated * mixed * sigma * (1.0 + gate * (1.0 - sigma))).astype(jnp.bfloat16)
+        kernel, offset = layer_kernel(layer)
+        act, conv_pull = jax.vjp(
+            lambda pad, ker, off: conv_apply(pad, seg_padded, ker, off), padded, kernel, offset
+        )
+        inner, bmat, cmat, step = split_act(act, layer)
+        decay = -jnp.exp(decay_log[layer])
+        flow = inflow(step, decay, seg_here, cont)
+        d_mixed3 = d_mixed.reshape(length, heads_local, head_size)
+        adjoint = jnp.einsum("th,thp,tn->hpn", flow, d_mixed3, cmat, precision=HIGH)
+        carried = passed_along(adjoint.astype(bf), "ctx", -1).astype(jnp.float32)
+
+        def mixer_local(inner_v, bmat_v, cmat_v, step_v, decay_v, skip_v, entry):
+            part_v, produced_v = ssd_block(
+                inner_v, bmat_v, cmat_v, step_v, decay_v, skip_v, seg_here, cont, zeros_state
+            )
+            flow_v = inflow(step_v, decay_v, seg_here, cont)
+            result_v = part_v + jnp.einsum("th,tn,hpn->thp", flow_v, cmat_v, entry, precision=HIGH)
+            return (result_v, flow_v[-1][:, None, None] * entry + produced_v)
+
+        _, ssd_pull = jax.vjp(
+            mixer_local, inner, bmat, cmat, step, decay, skip_gain[layer], incoming
+        )
+        g_inner, g_bmat, g_cmat, g_step, g_decay, skip_grad, _ = ssd_pull((d_mixed3, carried))
+        g_state = tp_sum(jnp.concatenate([g_bmat, g_cmat], 1).astype(bf), 4).astype(jnp.float32)
+        g_act = jnp.concatenate([g_inner.reshape(length, inner_local), g_state], 1)
+        g_padded, kernel_grad, offset_grad = conv_pull(g_act)
+        returned = passed_along(g_padded[: taps - 1], "ctx", -1)
+        g_raw = g_padded[taps - 1 :] + jnp.concatenate(
+            [jnp.zeros((length - (taps - 1), g_padded.shape[1]), jnp.float32), returned], 0
+        )
+        g_step_raw = g_step * jax.nn.sigmoid(kept_step[layer] + step_bias[layer])
+        g_inner_b = g_raw[:, :inner_local].astype(jnp.bfloat16)
+        g_state_b = g_raw[:, inner_local:].astype(jnp.bfloat16)
+        g_step_b = g_step_raw.astype(jnp.bfloat16)
+        blank = jnp.zeros((length, pad), bf)
+        delta = jnp.concatenate([d_gate, g_inner_b, g_state_b, g_step_b, blank], 1)
+        single = jnp.concatenate([d_gate, g_inner_b, g_state_b * lead, g_step_b, blank], 1)
+        d_normed = tp_sum(contract_cols(single, win[layer]).astype(bf), 5).astype(jnp.float32)
+        _, norm_pull = jax.vjp(rms_apply, hidden_in, prenorm[layer])
+        d_hidden, prenorm_full = norm_pull(d_normed)
+        prenorm_grad = lax.dynamic_slice_in_dim(prenorm_full, feat_start, feat)
+        shard_grads[layer] = (
+            grad_rows(normed, delta, feat_dim).astype(bf),
+            mixer_grad.astype(bf),
+        )
+        back = back + d_hidden
+        small_grads[layer] = (
+            prenorm_grad,
+            kernel_grad[:, :inner_local],
+            offset_grad[:inner_local],
+            kernel_grad[:, inner_local:],
+            offset_grad[inner_local:],
+            jnp.sum(g_step_raw, 0),
+            g_decay * decay,
+            skip_grad,
+            norm_grad,
+        )
+    output = lax.dynamic_slice_in_dim(output, feat_start, feat, 1)
+    back = lax.dynamic_slice_in_dim(back, feat_start, feat, 1)
+
+    def stack_member(groups, member):
+        return jnp.stack([groups[layer][member] for layer in range(layers)])
+
+    members = [stack_member(small_grads, member) for member in range(9)]
+    flat = jnp.concatenate([m.reshape(-1) for m in members])
+    fill = -flat.shape[0] % 1024
+    flat = jnp.concatenate([flat, jnp.zeros((fill,), jnp.float32)]).reshape(-1, 128)
+    grads = [piece for layer in range(layers) for piece in shard_grads[layer]]
+    gate_g, inner_g, extra_g, mixer_g, flat = reduce_grads(grads, flat)
+    flat = flat.reshape(-1)
+    summed, start = [], 0
+    for m in members:
+        summed.append(flat[start : start + m.size].reshape(m.shape))
+        start += m.size
+    return (
+        output,
+        back,
+        summed[0],
+        gate_g,
+        inner_g,
+        extra_g[:, :, : 2 * state_size],
+        extra_g[:, :, 2 * state_size : 2 * state_size + heads_local],
+        summed[1],
+        summed[2],
+        summed[3],
+        summed[4],
+        summed[5],
+        summed[6],
+        summed[7],
+        summed[8],
+        mixer_g,
+    )
+
+
+def pick(*args):
+    nz, ny, n = (lax.axis_size(name) for name in ("fsdp", "ctx", "tp"))
+    length, rows, cols = args[0].shape[0], args[4].shape[1], args[4].shape[2]
+    heads, states = args[7].shape[2], args[6].shape[2]
+    fits = ny == 2 and nz <= 4 and n > 1 and rows % 16 == 0 and cols % 128 == 0
+    fits = fits and length % (16 * n) == 0 and length % 128 == 0 and cols >= states + heads
+    return (body_kernels if fits else body)(*args)
+
+
 def solution(mesh):
     placed = (
         P(("fsdp", "ctx"), None),
@@ -423,7 +946,7 @@
         P(None, ("fsdp", "ctx"), "tp"),
     )
     return jax.shard_map(
-        body,
+        pick,
         mesh=mesh,
         in_specs=placed,
         out_specs=(

time: 1340 us -> 370 us (0.28)
  waiting for transfers between devices: 747 us -> 8.92 us
  blocking collectives: 413 us -> 0 us
  Pallas kernels: 0 us -> 198 us
  matrix products: 65.4 us -> 47.7 us
  local copies, waits for them, and re-layouts: 36.1 us -> 52.9 us
    reduce_scatter x8 -> x0, waiting for transfers between devices: 490 us -> none  [the longest x2 133 us: body(): lax.psum_scatter(mixer_grad, ('fsdp', 'ctx'), scatter_dimension=0, tiled=...]
    all_gather x16 -> x0, blocking collectives: 351 us -> none  [the longest x2 67.1 us: body(): lax.all_gather(gate_proj[layer], ('fsdp', 'ctx'), axis=0, tiled=True)]
    pallas_call x0 -> x8, Pallas kernels: none -> 198 us  [the longest x1 72 us: reduce_grads(): pl.pallas_call(functools.partial(grads_kernel, nz, layers), out_shape=tup...]
    psum x6 -> x0, waiting for transfers between devices: 144 us -> none  [the longest x2 63.2 us: body(): lax.psum(partial_normed.astype(jnp.bfloat16), 'tp').astype(jnp.float32)]
    unnamed x18 -> x0, waiting for transfers between devices: 106 us -> none
    psum x5 -> x0, blocking collectives: 62.2 us -> none  [the longest x1 38.1 us: body(): lax.psum((stack_member(small_grads, 0), stack_member(small_grads, 1), sta...]
  transfers between devices with their start and end apart: 20 -> 8, of which waited for: 17 -> 4; matrix products, arithmetic and copies ran while one was open for 4% -> 10% of each run, Pallas kernels for 0% -> 0%
where the time goes in v1:
time: 370 us; the launch traced here: 368 us
  Pallas kernels  198 us (54%)
  local copies, waits for them, and re-layouts  52.9 us (14%)
  matrix products  47.7 us (13%)
  other arithmetic  40.4 us (11%)
  starting transfers between devices  15.9 us (4%)
  waiting for transfers between devices  8.92 us (2%)
  between operations  4.56 us (1%)
    pallas_call x1, Pallas kernels, reduce_grads(): pl.pallas_call(functools.partial(grads_kernel, nz, layers), out_shape=tup...  72 us
    pallas_call x1, Pallas kernels, gather_weights(): pl.pallas_call(functools.partial(weights_kernel, nz, ny), out_shape=(jax....  69.3 us
    pallas_call x6, Pallas kernels, tp_sum(): pl.pallas_call(functools.partial(sum_kernel, n, tallied), out_shape=shape...  56.3 us
    ppermute x8, starting transfers between devices, passed_along(): return lax.ppermute(block, axis, route)  15.9 us
    dot_general x6, matrix products, advance(): jnp.einsum('tsh,shp->thp', weights * scores[:, :, None], scaled, precisio...  12.8 us
    unnamed x317, local copies, waits for them, and re-layouts  9.01 us
    ppermute x8, waiting for transfers between devices, passed_along(): return lax.ppermute(block, axis, route)  8.92 us
    dot_general x4, matrix products, contract_cols(): lax.dot_general(left, right, (((1,), (1,)), ((), ())), preferred_element_...  8.72 us
  transfers between devices with their start and end apart: 8, of which 4 were waited for; matrix products, arithmetic and copies ran while one was open for 10% of the time, Pallas kernels for 0%

profile of v1, /device:TPU:0, one launch (start us, length us, event | category | flops | bytes accessed | tf_op | source)
XLA Modules:
  0.0 368.0 jit_solution(12473942907937668131)
XLA Ops:
  3.4 1.6 maximum_maximum_fusion.refs_2_
  5.0 69.3 %weights.1 = (bf16[2,768,1152]{2,1,0:T(8,128)(2,1)}, bf16[2,768,384]{2,1,0:T(8,128)(2,1)}) custom-call(bf16[2,96,384]{2,1,0:T(8,128)(2,1)} %refs_0_.1, bf16[2,96,384]{2,1,0:T(8,128)(2,1)} %refs_1_.1, bf16[2,96,384]{2,1,0:T(8,128)(2,1)} %maximum_maximum_fusion.refs_2_, bf16[2,96,384]{2,1,0:T(8,128)(2,1)} %refs_3_.1), custom_call_target="tpu_custom_call" | custom-call | tf_op jit(solution)/shard_map/weights/pallas_call | solution.py:242
  74.3 2.1 fusion.237
  76.6 1.6 collective-permute-start
  82.4 1.4 compare_convert_fusion
  92.7 1.3 collective-permute-start.1
  94.3 1.9 collective-permute-done.1
  96.5 2.4 multiply_add_fusion.7
  101.8 10.5 %tpsum.6 = (bf16[128,768]{1,0:T(8,128)(2,1)}, f32[8,128]{1,0:T(8,128)}) custom-call(bf16[128,768]{1,0:T(8,128)(2,1)} %convolution_convert_fusion.5.refs_0_, f32[8,128]{1,0:T(8,128)} %broadcast_in_dim.425.refs_1_), custom_call_target="tpu_custom_call" | custom-call | tf_op jit(solution)/shard_map/tpsum/pallas_call | solution.py:447
  113.0 1.2 multiply_reduce_fusion.4
  114.3 2.0 fusion.238
  117.7 4.3 %collective-permute-start.2 = (bf16[3,640]{1,0:T(4,128)(2,1)S(1)}, bf16[3,640]{1,0:T(4,128)(2,1)S(1)}, u32[]{:S(2)}, u32[]{:S(2)}) collective-permute-start(bf16[3,640]{1,0:T(4,128)(2,1)S(1)} %slice.548), channel_id=1, source_target_pairs={{0,4},{1,5},{2,6},{3,7},{8,12},{9,13},{10,14},{11,15},{16,20},{17,... | collective-permute-start | bytes 11528 | tf_op jit(solution)/shard_map/ppermute | solution.py:20
  126.3 3.2 collective-permute-start.3
  129.8 1.9 collective-permute-done.3
  132.0 2.4 multiply_add_fusion.6
  135.5 1.1 multiply_reduce_fusion.26
  136.6 2.1 convolution_convert_fusion.4.refs_0_
  139.3 9.6 %tpsum.7 = (bf16[128,768]{1,0:T(8,128)(2,1)}, f32[8,128]{1,0:T(8,128)}) custom-call(bf16[128,768]{1,0:T(8,128)(2,1)} %convolution_convert_fusion.4.refs_0_, f32[8,128]{1,0:T(8,128)} %broadcast_in_dim.426.refs_1_), custom_call_target="tpu_custom_call" | custom-call | tf_op jit(solution)/shard_map/tpsum/pallas_call | solution.py:447
  148.9 1.8 convert_element_type.282
  150.7 1.1 multiply_reduce_fusion.3
  153.1 1.9 fusion.12.refs_3_
  155.0 2.6 multiply_reduce_fusion.18
  157.6 1.1 copy.267
  158.7 1.6 convolution_convert_fusion.7
  160.3 1.5 collective-permute-start.4
  161.8 2.4 fusion.66
  165.1 1.7 dynamic-slice_add_fusion
  166.9 1.1 multiply_reduce_fusion.15
  169.4 1.4 copy.281
  170.8 1.3 stack.88
  173.5 1.6 copy.313
  175.4 2.7 multiply_reduce_fusion.24
  178.2 1.7 copy.269
  179.9 1.9 multiply_add_fusion.5
  181.8 1.7 copy.273
  183.6 1.4 convolution_bitcast_fusion.14
  188.1 8.7 %tpsum.8 = bf16[128,256]{1,0:T(8,128)(2,1)} custom-call(bf16[128,256]{1,0:T(8,128)(2,1)} %pad_maximum_fusion.2.refs_0_), custom_call_target="tpu_custom_call" | custom-call | tf_op jit(solution)/shard_map/tpsum/pallas_call | solution.py:447
  197.7 1.4 multiply_reduce_fusion.9
  200.6 1.1 reduce_window_sum.93
  201.8 1.1 reduce_window_sum.92
  203.0 1.3 collective-permute-start.5
  207.0 1.6 collective-permute-done.5
  208.9 2.8 fusion.16.refs_0_
  211.8 9.5 %tpsum.9 = bf16[128,768]{1,0:T(8,128)(2,1)} custom-call(bf16[128,768]{1,0:T(8,128)(2,1)} %fusion.16.refs_0_), custom_call_target="tpu_custom_call" | custom-call | tf_op jit(solution)/shard_map/tpsum/pallas_call | solution.py:447
  221.3 1.2 fusion.47
  222.5 1.2 fusion.46
  224.4 1.2 convolution_convert_fusion.3.refs_1_
  225.7 1.3 multiply_reduce_fusion.19
  228.9 1.5 collective-permute-start.6
  230.5 1.6 fusion.68
  233.0 2.0 convolution_convert_fusion.refs_2_
  238.2 1.2 multiply_reduce_fusion.21
  241.9 8.6 %tpsum.10 = bf16[128,256]{1,0:T(8,128)(2,1)} custom-call(bf16[128,256]{1,0:T(8,128)(2,1)} %pad_maximum_fusion.3.refs_0_), custom_call_target="tpu_custom_call" | custom-call | tf_op jit(solution)/shard_map/tpsum/pallas_call | solution.py:447
  253.4 1.1 reduce_window_sum.95
  254.6 1.1 reduce_window_sum.94
  255.8 1.3 collective-permute-start.7
  257.9 3.5 collective-permute-done.7
  261.7 2.8 fusion.13.refs_0_
  264.5 9.5 %tpsum.11 = bf16[128,768]{1,0:T(8,128)(2,1)} custom-call(bf16[128,768]{1,0:T(8,128)(2,1)} %fusion.13.refs_0_), custom_call_target="tpu_custom_call" | custom-call | tf_op jit(solution)/shard_map/tpsum/pallas_call | solution.py:447
  274.0 1.1 fusion.48
  275.3 2.0 convolution_convert_fusion.1.refs_0_
  277.9 72.0 %grads.1 = (f32[2,96,384]{2,1,0:T(8,128)}, f32[2,96,384]{2,1,0:T(8,128)}, f32[2,96,384]{2,1,0:T(8,128)}, f32[2,96,384]{2,1,0:T(8,128)}, f32[64,128]{1,0:T(8,128)}) custom-call(bf16[768,1152]{1,0:T(8,128)(2,1)} %convolution_convert_fusion.1.refs_0_, bf16[768,384]{1,0:T(8,128)(2,1)} %convolution_convert_fusion.3.refs_1_, ...), custom_call_target="tpu_custom_call" | custom-call | tf_op jit(solution)/shard_map/grads/pallas_call | solution.py:361
  350.0 1.7 slice.515
  364.0 1.1 fusion.120
  (542 shorter events, 68.6 us)
Async XLA Ops:
  2.5 73.9 %copy-start.96 = (f32[128]{0:T(128)}, f32[128]{0:T(128)S(1)}, u32[]{:S(2)}) copy-start(f32[128]{0:T(128)S(1)} %fusion.212) | copy-start | bytes 1540
  5.0 73.2 %copy-start.145 = (s32[1,256]{1,0:T(1,128)S(1)}, s32[1,256]{1,0:T(1,128)}, u32[]{:S(2)}) copy-start(s32[1,256]{1,0:T(1,128)} %param.18) | copy-start | bytes 3076
  74.3 10.4 %copy-start = (bf16[128,768]{1,0:T(8,128)(2,1)S(1)}, bf16[128,768]{1,0:T(8,128)(2,1)}, u32[]{:S(2)}) copy-start(bf16[128,768]{1,0:T(8,128)(2,1)} %param.17) | copy-start | bytes 589828
  74.3 11.2 %copy-start.95 = (f32[2,4,384]{2,1,0:T(4,128)S(1)}, f32[2,4,384]{2,1,0:T(4,128)}, u32[]{:S(2)}) copy-start(f32[2,4,384]{2,1,0:T(4,128)} %param.25) | copy-start | bytes 36868
  76.5 23.6 %copy-start.4 = (f32[128,1152]{1,0:T(8,128)}, f32[128,1152]{1,0:T(8,128)S(1)}, u32[]{:S(2)}) copy-start(f32[128,1152]{1,0:T(8,128)S(1)} %get-tuple-element.883) | copy-start | bytes 1769476
  76.5 9.0 %copy-start.100 = (f32[2,4,256]{2,1,0:T(4,128)S(1)}, f32[2,4,256]{2,1,0:T(4,128)}, u32[]{:S(2)}) copy-start(f32[2,4,256]{2,1,0:T(4,128)} %param.27) | copy-start | bytes 24580
  76.5 9.1 %copy-start.137 = (f32[2,256]{1,0:T(2,128)S(1)}, f32[2,256]{1,0:T(2,128)}, u32[]{:S(2)}) copy-start(f32[2,256]{1,0:T(2,128)} %param.28) | copy-start | bytes 6148
  76.5 9.8 %copy-start.146 = (f32[2,6]{1,0:T(2,128)S(1)}, f32[2,6]{1,0:T(2,128)}, u32[]{:S(2)}) copy-start(f32[2,6]{1,0:T(2,128)} %param.31) | copy-start | bytes 148
  76.5 9.8 %copy-start.132 = (f32[2,384]{1,0:T(2,128)S(1)}, f32[2,384]{1,0:T(2,128)}, u32[]{:S(2)}) copy-start(f32[2,384]{1,0:T(2,128)} %param.32) | copy-start | bytes 9220
  76.6 14.2 %collective-permute-start = (bf16[3,640]{1,0:T(4,128)(2,1)S(1)}, bf16[3,640]{1,0:T(4,128)(2,1)S(1)}, u32[]{:S(2)}, u32[]{:S(2)}) collective-permute-start(bf16[3,640]{1,0:T(4,128)(2,1)S(1)} %slice.529), channel_id=1, source_target_pairs={{0,4},{1,5},{2,6},{3,7},{8,12},{9,13},{10,14},{11,15},{16,20},{17,... | collective-permute-start | bytes 11528 | tf_op jit(solution)/shard_map/ppermute | solution.py:20
  82.1 14.4 %copy-start.38 = (f32[128,6]{0,1:T(8,128)}, f32[128,6]{0,1:T(8,128)S(1)}, u32[]{:S(2)}) copy-start(f32[128,6]{0,1:T(8,128)S(1)} %get-tuple-element.819) | copy-start | bytes 9220
  83.8 40.6 %copy-start.65 = (f32[128]{0:T(128)}, f32[128]{0:T(128)S(1)}, u32[]{:S(2)}) copy-start(f32[128]{0:T(128)S(1)} %get-tuple-element.868) | copy-start | bytes 1540
  83.8 40.6 %copy-start.68 = (f32[128]{0:T(128)}, f32[128]{0:T(128)S(1)}, u32[]{:S(2)}) copy-start(f32[128]{0:T(128)S(1)} %get-tuple-element.869) | copy-start | bytes 1540
  84.0 12.5 %copy-start.34 = (f32[128,6]{0,1:T(8,128)}, f32[128,6]{0,1:T(8,128)S(1)}, u32[]{:S(2)}) copy-start(f32[128,6]{0,1:T(8,128)S(1)} %copy.254) | copy-start | bytes 9220
  90.7 33.7 %copy-start.53 = (f32[640]{0:T(1024)}, f32[640]{0:T(1024)S(1)}, u32[]{:S(2)}) copy-start(f32[640]{0:T(1024)S(1)} %get-tuple-element.778) | copy-start | bytes 7684
  90.7 33.7 %copy-start.55 = (f32[640]{0:T(1024)}, f32[640]{0:T(1024)S(1)}, u32[]{:S(2)}) copy-start(f32[640]{0:T(1024)S(1)} %get-tuple-element.779) | copy-start | bytes 7684
  90.7 33.7 %copy-start.57 = (f32[640]{0:T(1024)}, f32[640]{0:T(1024)S(1)}, u32[]{:S(2)}) copy-start(f32[640]{0:T(1024)S(1)} %get-tuple-element.780) | copy-start | bytes 7684
  90.8 33.7 %copy-start.59 = (f32[640]{0:T(1024)}, f32[640]{0:T(1024)S(1)}, u32[]{:S(2)}) copy-start(f32[640]{0:T(1024)S(1)} %get-tuple-element.781) | copy-start | bytes 7684
  92.7 3.5 collective-permute-start.1
  96.2 16.1 %copy-start.8 = (bf16[6,64,128]{2,1,0:T(8,128)(2,1)}, bf16[6,64,128]{2,1,0:T(8,128)(2,1)S(1)}, u32[]{:S(2)}) copy-start(bf16[6,64,128]{2,1,0:T(8,128)(2,1)S(1)} %collective-permute-done.1) | copy-start | bytes 294916
  100.0 13.0 %copy-start.11 = (f32[128,384]{1,0:T(8,128)}, f32[128,384]{1,0:T(8,128)S(1)}, u32[]{:S(2)}) copy-start(f32[128,384]{1,0:T(8,128)S(1)} %copy.256) | copy-start | bytes 589828
  117.2 14.8 %copy-start.40 = (f32[128,6]{0,1:T(8,128)}, f32[128,6]{0,1:T(8,128)S(1)}, u32[]{:S(2)}) copy-start(f32[128,6]{0,1:T(8,128)S(1)} %get-tuple-element.811) | copy-start | bytes 9220
  117.7 6.7 %collective-permute-start.2 = (bf16[3,640]{1,0:T(4,128)(2,1)S(1)}, bf16[3,640]{1,0:T(4,128)(2,1)S(1)}, u32[]{:S(2)}, u32[]{:S(2)}) collective-permute-start(bf16[3,640]{1,0:T(4,128)(2,1)S(1)} %slice.548), channel_id=1, source_target_pairs={{0,4},{1,5},{2,6},{3,7},{8,12},{9,13},{10,14},{11,15},{16,20},{17,... | collective-permute-start | bytes 11528 | tf_op jit(solution)/shard_map/ppermute | solution.py:20
  122.1 9.9 %copy-start.36 = (f32[128,6]{0,1:T(8,128)}, f32[128,6]{0,1:T(8,128)S(1)}, u32[]{:S(2)}) copy-start(f32[128,6]{0,1:T(8,128)S(1)} %copy.262) | copy-start | bytes 9220
  126.3 5.4 %collective-permute-start.3 = (bf16[6,64,128]{2,1,0:T(8,128)(2,1)S(1)}, bf16[6,64,128]{2,1,0:T(8,128)(2,1)S(1)}, u32[]{:S(2)}, u32[]{:S(2)}) collective-permute-start(bf16[6,64,128]{2,1,0:T(8,128)(2,1)S(1)} %fusion.24), channel_id=1, source_target_pairs={{0,4},{1,5},{2,6},{3,7},{8,12},{9,13},{10,14},{11,15},{16,20},{17,... | collective-permute-start | bytes 294920 | tf_op jit(solution)/shard_map/ppermute | solution.py:20
  132.0 18.7 %copy-start.1 = (f32[128,768]{1,0:T(8,128)S(1)}, f32[128,768]{1,0:T(8,128)}, u32[]{:S(2)}) copy-start(f32[128,768]{1,0:T(8,128)} %param.19) | copy-start | bytes 1179652
  160.3 14.8 %collective-permute-start.4 = (bf16[6,64,128]{2,1,0:T(8,128)(2,1)}, bf16[6,64,128]{2,1,0:T(8,128)(2,1)S(1)}, u32[]{:S(2)}, u32[]{:S(2)}) collective-permute-start(bf16[6,64,128]{2,1,0:T(8,128)(2,1)} %convolution_convert_fusion.7), channel_id=1, source_target_pairs={{4,0},{5,1},{6,2},{7,3},{12,8},{13,9},{14,10},{15,11},{20,16},{21,... | collective-permute-start | bytes 294920 | tf_op jit(solution)/shard_map/ppermute | solution.py:20
  161.8 13.6 %copy-start.41 = (f32[128,6]{0,1:T(8,128)S(1)}, f32[128,6]{0,1:T(8,128)}, u32[]{:S(2)}) copy-start(f32[128,6]{0,1:T(8,128)} %copy-done.40) | copy-start | bytes 9220
  161.8 13.6 %copy-start.81 = (f32[128,6]{0,1:T(8,128)S(1)}, f32[128,6]{0,1:T(8,128)}, u32[]{:S(2)}) copy-start(f32[128,6]{0,1:T(8,128)} %copy.268) | copy-start | bytes 9220
  161.8 13.6 %copy-start.84 = (pred[128,128]{1,0:T(8,128)(4,1)S(1)}, pred[128,128]{1,0:T(8,128)(4,1)}, u32[]{:S(2)}) copy-start(pred[128,128]{1,0:T(8,128)(4,1)} %fusion.161) | copy-start | bytes 49156
  168.7 11.2 %copy-start.99 = (f32[384]{0:T(512)S(1)}, f32[384]{0:T(512)}, u32[]{:S(2)}) copy-start(f32[384]{0:T(512)} %mul.1743) | copy-start | bytes 4612
  175.4 11.7 %copy-start.37 = (f32[128,6]{0,1:T(8,128)S(1)}, f32[128,6]{0,1:T(8,128)}, u32[]{:S(2)}) copy-start(f32[128,6]{0,1:T(8,128)} %copy-done.36) | copy-start | bytes 9220
  178.2 19.5 %copy-start.66 = (f32[128]{0:T(128)S(1)}, f32[128]{0:T(128)}, u32[]{:S(2)}) copy-start(f32[128]{0:T(128)} %copy-done.65) | copy-start | bytes 1540
  178.2 19.5 %copy-start.69 = (f32[128]{0:T(128)S(1)}, f32[128]{0:T(128)}, u32[]{:S(2)}) copy-start(f32[128]{0:T(128)} %copy-done.68) | copy-start | bytes 1540
  186.0 13.1 %copy-start.54 = (f32[640]{0:T(1024)S(1)}, f32[640]{0:T(1024)}, u32[]{:S(2)}) copy-start(f32[640]{0:T(1024)} %copy-done.53) | copy-start | bytes 7684
  186.0 13.1 %copy-start.56 = (f32[640]{0:T(1024)S(1)}, f32[640]{0:T(1024)}, u32[]{:S(2)}) copy-start(f32[640]{0:T(1024)} %copy-done.55) | copy-start | bytes 7684
  186.0 13.1 %copy-start.58 = (f32[640]{0:T(1024)S(1)}, f32[640]{0:T(1024)}, u32[]{:S(2)}) copy-start(f32[640]{0:T(1024)} %copy-done.57) | copy-start | bytes 7684
  186.1 13.1 %copy-start.60 = (f32[640]{0:T(1024)S(1)}, f32[640]{0:T(1024)}, u32[]{:S(2)}) copy-start(f32[640]{0:T(1024)} %copy-done.59) | copy-start | bytes 7684
  187.1 12.0 %copy-start.73 = (f32[128]{0:T(128)S(1)}, f32[128]{0:T(128)}, u32[]{:S(2)}) copy-start(f32[128]{0:T(128)} %copy-done.71) | copy-start | bytes 1540
  199.4 9.3 %copy-start.20 = (bf16[128,384]{1,0:T(8,128)(2,1)S(1)}, bf16[128,384]{1,0:T(8,128)(2,1)}, u32[]{:S(2)}) copy-start(bf16[128,384]{1,0:T(8,128)(2,1)} %get-tuple-element.823) | copy-start | bytes 294916
  203.0 5.6 %collective-permute-start.5 = (f32[3,640]{1,0:T(4,128)S(1)}, f32[3,640]{1,0:T(4,128)S(1)}, u32[]{:S(2)}, u32[]{:S(2)}) collective-permute-start(f32[3,640]{1,0:T(4,128)S(1)} %pad_add_fusion.3), channel_id=1, source_target_pairs={{4,0},{5,1},{6,2},{7,3},{12,8},{13,9},{14,10},{15,11},{20,16},{21,... | collective-permute-start | bytes 23048 | tf_op jit(solution)/shard_map/ppermute | solution.py:20
  208.8 12.5 %copy-start.102 = (f32[128]{0:T(128)S(1)}, f32[128]{0:T(128)}, u32[]{:S(2)}) copy-start(f32[128]{0:T(128)} %copy-done.101) | copy-start | bytes 1540
  208.9 13.6 %copy-start.151 = (f32[128]{0:T(128)S(1)}, f32[128]{0:T(128)}, u32[]{:S(2)}) copy-start(f32[128]{0:T(128)} %copy-done.150) | copy-start | bytes 1540
  208.9 13.6 %copy-start.10 = (bf16[128,768]{1,0:T(8,128)(2,1)S(1)}, bf16[128,768]{1,0:T(8,128)(2,1)}, u32[]{:S(2)}) copy-start(bf16[128,768]{1,0:T(8,128)(2,1)} %get-tuple-element.657) | copy-start | bytes 589828
  211.8 12.6 %copy-start.77 = (f32[384]{0:T(512)S(1)}, f32[384]{0:T(512)}, u32[]{:S(2)}) copy-start(f32[384]{0:T(512)} %get-tuple-element.793) | copy-start | bytes 4612
  211.8 12.6 %copy-start.134 = (f32[128]{0:T(128)S(1)}, f32[128]{0:T(128)}, u32[]{:S(2)}) copy-start(f32[128]{0:T(128)} %copy-done.133) | copy-start | bytes 1540
  228.9 9.0 %collective-permute-start.6 = (bf16[6,64,128]{2,1,0:T(8,128)(2,1)S(1)}, bf16[6,64,128]{2,1,0:T(8,128)(2,1)S(1)}, u32[]{:S(2)}, u32[]{:S(2)}) collective-permute-start(bf16[6,64,128]{2,1,0:T(8,128)(2,1)S(1)} %convolution_convert_fusion.6), channel_id=1, source_target_pairs={{4,0},{5,1},{6,2},{7,3},{12,8},{13,9},{14,10},{15,11},{20,16},{21,... | collective-permute-start | bytes 294920 | tf_op jit(solution)/shard_map/ppermute | solution.py:20
  239.4 12.0 %copy-start.2 = (f32[128,640]{1,0:T(8,128)S(1)}, f32[128,640]{1,0:T(8,128)}, u32[]{:S(2)}) copy-start(f32[128,640]{1,0:T(8,128)} %get-tuple-element.821) | copy-start | bytes 983044
  239.4 12.0 %copy-start.67 = (f32[128]{0:T(128)S(1)}, f32[128]{0:T(128)}, u32[]{:S(2)}) copy-start(f32[128]{0:T(128)} %copy-done.65) | copy-start | bytes 1540
  239.4 12.0 %copy-start.70 = (f32[128]{0:T(128)S(1)}, f32[128]{0:T(128)}, u32[]{:S(2)}) copy-start(f32[128]{0:T(128)} %copy-done.68) | copy-start | bytes 1540
  239.4 12.0 %copy-start.74 = (f32[128]{0:T(128)S(1)}, f32[128]{0:T(128)}, u32[]{:S(2)}) copy-start(f32[128]{0:T(128)} %copy-done.71) | copy-start | bytes 1540
  240.5 11.4 %copy-start.46 = (f32[640]{0:T(1024)S(1)}, f32[640]{0:T(1024)}, u32[]{:S(2)}) copy-start(f32[640]{0:T(1024)} %copy-done.45) | copy-start | bytes 7684
  240.5 11.4 %copy-start.48 = (f32[640]{0:T(1024)S(1)}, f32[640]{0:T(1024)}, u32[]{:S(2)}) copy-start(f32[640]{0:T(1024)} %copy-done.47) | copy-start | bytes 7684
  240.5 11.4 %copy-start.50 = (f32[640]{0:T(1024)S(1)}, f32[640]{0:T(1024)}, u32[]{:S(2)}) copy-start(f32[640]{0:T(1024)} %copy-done.49) | copy-start | bytes 7684
  240.5 11.4 %copy-start.52 = (f32[640]{0:T(1024)S(1)}, f32[640]{0:T(1024)}, u32[]{:S(2)}) copy-start(f32[640]{0:T(1024)} %copy-done.51) | copy-start | bytes 7684
  255.8 5.6 %collective-permute-start.7 = (f32[3,640]{1,0:T(4,128)S(1)}, f32[3,640]{1,0:T(4,128)S(1)}, u32[]{:S(2)}, u32[]{:S(2)}) collective-permute-start(f32[3,640]{1,0:T(4,128)S(1)} %pad_add_fusion.2), channel_id=1, source_target_pairs={{4,0},{5,1},{6,2},{7,3},{12,8},{13,9},{14,10},{15,11},{20,16},{21,... | collective-permute-start | bytes 23048 | tf_op jit(solution)/shard_map/ppermute | solution.py:20
  261.6 12.4 %copy-start.97 = (f32[128]{0:T(128)S(1)}, f32[128]{0:T(128)}, u32[]{:S(2)}) copy-start(f32[128]{0:T(128)} %copy-done.96) | copy-start | bytes 1540
  261.7 13.5 %copy-start.128 = (f32[192]{0:T(256)S(1)}, f32[192]{0:T(256)}, u32[]{:S(2)}) copy-start(f32[192]{0:T(256)} %dynamic-slice.23) | copy-start | bytes 2308
  264.5 12.7 %copy-start.83 = (f32[768]{0:T(1024)S(1)}, f32[768]{0:T(1024)}, u32[]{:S(2)}) copy-start(f32[768]{0:T(1024)} %reshape.1370) | copy-start | bytes 9220
  264.5 12.7 %copy-start.152 = (f32[12]{0:T(128)S(1)}, f32[12]{0:T(128)}, u32[]{:S(2)}) copy-start(f32[12]{0:T(128)} %reshape.1369) | copy-start | bytes 148
  277.9 86.0 %copy-start.149 = (f32[128]{0:T(128)S(1)}, f32[128]{0:T(128)}, u32[]{:S(2)}) copy-start(f32[128]{0:T(128)} %copy-done.148) | copy-start | bytes 1540
  350.0 15.9 %copy-start.23 = (f32[2,96,384]{2,1,0:T(8,128)S(1)}, f32[2,96,384]{2,1,0:T(8,128)}, u32[]{:S(2)}) copy-start(f32[2,96,384]{2,1,0:T(8,128)} %get-tuple-element.915) | copy-start | bytes 884740
  350.0 16.6 %copy-start.22 = (f32[2,96,384]{2,1,0:T(8,128)S(1)}, f32[2,96,384]{2,1,0:T(8,128)}, u32[]{:S(2)}) copy-start(f32[2,96,384]{2,1,0:T(8,128)} %get-tuple-element.916) | copy-start | bytes 884740
  350.0 17.3 %copy-start.21 = (f32[2,96,384]{2,1,0:T(8,128)S(1)}, f32[2,96,384]{2,1,0:T(8,128)}, u32[]{:S(2)}) copy-start(f32[2,96,384]{2,1,0:T(8,128)} %get-tuple-element.927) | copy-start | bytes 884740
  (98 other events, 411.4 us)

commit v2 on v1

--- a/solution.py
+++ b/solution.py
@@ -455,6 +455,122 @@
     )(*((x, tally) if tallied else (x,)))
 
 
+def dots(left, right, dims):
+    return lax.dot_general(
+        left, right, (dims, ((), ())), precision=HIGH, preferred_element_type=jnp.float32
+    )
+
+
+def scan_parts(x_ref, bc_ref, step_ref, sd_ref, sdt_ref, aux_ref, row_ref):
+    length, width = x_ref.shape
+    heads = step_ref.shape[1]
+    size = width // heads
+    states = bc_ref.shape[1] // 2
+    order = lambda dim: lax.broadcasted_iota(jnp.int32, (length, length), dim)
+    lower = order(0) >= order(1)
+    upper = (order(0) <= order(1)).astype(jnp.float32)
+    spread = (
+        lax.broadcasted_iota(jnp.int32, (heads, width), 1) // size
+        == lax.broadcasted_iota(jnp.int32, (heads, width), 0)
+    ).astype(jnp.float32)
+    rep = lambda v: dots(v, spread, ((1,), (0,)))
+    logs = dots(lower.astype(jnp.float32), sd_ref[...], ((1,), (0,)))
+    logs_row = dots(sdt_ref[...], upper, ((1,), (0,)))
+    aux = aux_ref[...]
+    allowed = lower & (aux[:, 0:1] == row_ref[...])
+    into = aux[:, 1:2] * jnp.exp(logs)
+    tail = jnp.exp(logs[length - 1 : length, :] - logs) * aux[:, 2:3]
+    bmat, cmat = bc_ref[:, :states], bc_ref[:, states:]
+    scores = dots(cmat, bmat, ((1,), (1,)))
+
+    def weights(h):
+        gap = logs[:, h : h + 1] - logs_row[h : h + 1, :]
+        return jnp.where(allowed, jnp.exp(jnp.where(allowed, gap, 0.0)), 0.0)
+
+    scaled = x_ref[...] * rep(step_ref[...])
+    return heads, size, spread, rep, upper, into, tail, bmat, cmat, scores, weights, scaled
+
+
+def scan_kernel(x_ref, bc_ref, step_ref, sd_ref, sdt_ref, aux_ref, row_ref, skip_ref, y_ref, made_ref, into_ref):
+    heads, size, _, rep, _, into, tail, bmat, _, scores, weights, scaled = scan_parts(
+        x_ref, bc_ref, step_ref, sd_ref, sdt_ref, aux_ref, row_ref
+    )
+    into_ref[...] = into
+    made_ref[...] = dots(scaled * rep(tail), bmat, ((0,), (0,)))
+    for h in range(heads):
+        at = slice(h * size, (h + 1) * size)
+        local = dots(weights(h) * scores, scaled[:, at], ((1,), (0,)))
+        y_ref[:, at] = local + skip_ref[:, at] * x_ref[:, at]
+
+
+def back_kernel(
+    x_ref, bc_ref, step_ref, sd_ref, sdt_ref, aux_ref, row_ref, skip_ref, decay_ref, dm_ref,
+    mixed_ref, enter_ref, leave_ref, dx_ref, dbc_ref, dstep_ref, ddecay_ref, dskip_ref, local_ref,
+):
+    heads, size, spread, rep, upper, into, tail, bmat, cmat, scores, weights, scaled = scan_parts(
+        x_ref, bc_ref, step_ref, sd_ref, sdt_ref, aux_ref, row_ref
+    )
+    length, states = bmat.shape
+    fold = lambda v: dots(v, spread, ((1,), (1,)))
+    x, dm, enter, leave = x_ref[...], dm_ref[...], enter_ref[...], leave_ref[...]
+    skip = skip_ref[...]
+    tails = rep(tail)
+    from_state = tails * dots(bmat, leave, ((1,), (1,)))
+    d_scores = jnp.zeros((length, length), jnp.float32)
+    for h in range(heads):
+        at = slice(h * size, (h + 1) * size)
+        weight = weights(h)
+        dm_h = dm_ref[:, at]
+        d_scores += weight * dots(dm_h, scaled[:, at], ((1,), (1,)))
+        local_ref[:, at] = dots(weight * scores, dm_h, ((0,), (0,)))
+    dbc_ref[:, :states] = dots(scaled * tails, leave, ((1,), (0,))) + dots(
+        d_scores, cmat, ((0,), (0,))
+    )
+    dbc_ref[:, states:] = dots(dm * rep(into), enter, ((1,), (0,))) + dots(
+        d_scores, bmat, ((1,), (0,))
+    )
+    d_scaled = local_ref[...] + from_state
+    dx_ref[...] = d_scaled * rep(step_ref[...]) + skip * dm
+    d_logs = fold(dm * (mixed_ref[...] - skip * x) - scaled * d_scaled)
+    ones = jnp.ones((8, states), jnp.float32)
+    passed = fold(dots(ones, enter * leave, ((1,), (1,))))[0:1, :]
+    last = fold(jnp.sum(scaled * from_state, 0, keepdims=True))
+    last = last + into[length - 1 : length, :] * passed
+    rest = dots(upper, d_logs, ((1,), (0,))) + last
+    dstep_ref[...] = fold(d_scaled * x) + rest * decay_ref[...]
+    ddecay_ref[...] = jnp.sum(rest * step_ref[...], 0, keepdims=True)
+    dskip_ref[...] = jnp.sum(dm * x, 0, keepdims=True)
+
+
+def scan_forward(parts):
+    length, width = parts[0].shape
+    heads, states = parts[2].shape[1], parts[1].shape[1] // 2
+    f32 = lambda *shape: jax.ShapeDtypeStruct(shape, jnp.float32)
+    return pl.pallas_call(
+        scan_kernel,
+        out_shape=(f32(length, width), f32(width, states), f32(length, heads)),
+        in_specs=[VM] * len(parts),
+        out_specs=(VM,) * 3,
+        name="scan_forward",
+    )(*parts)
+
+
+def scan_backward(parts):
+    length, width = parts[0].shape
+    heads, states = parts[2].shape[1], parts[1].shape[1] // 2
+    f32 = lambda *shape: jax.ShapeDtypeStruct(shape, jnp.float32)
+    return pl.pallas_call(
+        back_kernel,
+        out_shape=(
+            f32(length, width), f32(length, 2 * states), f32(length, heads), f32(1, heads), f32(1, width),
+        ),
+        in_specs=[VM] * len(parts),
+        out_specs=(VM,) * 5,
+        scratch_shapes=[pltpu.VMEM((length, width), jnp.float32)],
+        name="scan_backward",
+    )(*parts)
+
+
 def body(
     tokens,
     segments,
@@ -707,6 +823,12 @@
     )
 
 
+def contract_high(left, right, left_dim, right_dim):
+    return lax.dot_general(
+        left, right, (((left_dim,), (right_dim,)), ((), ())), precision=HIGH
+    )
+
+
 def body_kernels(
     tokens,
     segments,
@@ -769,6 +891,16 @@
     )
     win, wmix = gather_weights(gate_proj, inner_proj, extra, mixer_out)
     bf = jnp.bfloat16
+    fresh = fresh_flags(seg_here, cont)
+    aux = jnp.stack(
+        [
+            seg_here.astype(jnp.float32),
+            (jnp.cumsum(fresh) == 0.0).astype(jnp.float32),
+            (seg_here == seg_here[-1]).astype(jnp.float32),
+        ],
+        1,
+    )
+    seg_row = seg_here.astype(jnp.float32)[None]
     lead = (lax.axis_index("tp") == 0).astype(bf)
     for layer in range(layers):
         inverse = None
@@ -782,15 +914,23 @@
         padded = jnp.concatenate([before, raw], 0).astype(jnp.float32)
         kernel, offset = layer_kernel(layer)
         act = conv_apply(padded, seg_padded, kernel, offset)
-        inner, bmat, cmat, step = split_act(act, layer)
         decay = -jnp.exp(decay_log[layer])
-        partial_mixed, produced = ssd_block(
-            inner, bmat, cmat, step, decay, skip_gain[layer], seg_here, cont, zeros_state
-        )
-        flow = inflow(step, decay, seg_here, cont)
+        step = jax.nn.softplus(step_raw + step_bias[layer])
+        marks = step * decay
+        parts = (
+            act[:, :inner_local],
+            act[:, inner_local:],
+            step,
+            marks,
+            marks.T,
+            aux,
+            seg_row,
+            jnp.repeat(skip_gain[layer], head_size)[None],
+        )
+        partial_mixed, produced, flow = scan_forward(parts)
         incoming = passed_along(produced.astype(bf), "ctx", 1).astype(jnp.float32)
-        mixed = partial_mixed + jnp.einsum("th,tn,hpn->thp", flow, cmat, incoming, precision=HIGH)
-        mixed = mixed.reshape(length, inner_local)
+        reach = contract_high(act[:, inner_local + state_size :], incoming, 1, 1)
+        mixed = partial_mixed + jnp.repeat(flow, head_size, axis=1) * reach
         gated = mixed * jax.nn.silu(gate)
         squares = jnp.broadcast_to(jnp.sum(gated * gated, 1)[None], (8, length))
         lifted = (gated * norm_gain[layer]).astype(bf)
@@ -800,7 +940,7 @@
         normout = (gated * scale[:, None] * norm_gain[layer]).astype(bf)
         stored = projected
         kept.append(
-            (hidden, inverse, stored, normed, gate, padded, incoming, mixed, gated, scale, normout)
+            (hidden, (parts, flow, decay), stored, normed, gate, padded, incoming, mixed, gated, scale, normout)
         )
         hidden = hidden + projected * scale[:, None]
     output = hidden
@@ -823,29 +963,19 @@
         d_mixed = d_gated * gate * sigma
         d_gate = (d_gated * mixed * sigma * (1.0 + gate * (1.0 - sigma))).astype(jnp.bfloat16)
         kernel, offset = layer_kernel(layer)
-        act, conv_pull = jax.vjp(
+        parts, flow, decay = inverse
+        _, conv_pull = jax.vjp(
             lambda pad, ker, off: conv_apply(pad, seg_padded, ker, off), padded, kernel, offset
         )
-        inner, bmat, cmat, step = split_act(act, layer)
-        decay = -jnp.exp(decay_log[layer])
-        flow = inflow(step, decay, seg_here, cont)
-        d_mixed3 = d_mixed.reshape(length, heads_local, head_size)
-        adjoint = jnp.einsum("th,thp,tn->hpn", flow, d_mixed3, cmat, precision=HIGH)
+        cmat = parts[1][:, state_size:]
+        adjoint = contract_high(jnp.repeat(flow, head_size, axis=1) * d_mixed, cmat, 0, 0)
         carried = passed_along(adjoint.astype(bf), "ctx", -1).astype(jnp.float32)
-
-        def mixer_local(inner_v, bmat_v, cmat_v, step_v, decay_v, skip_v, entry):
-            part_v, produced_v = ssd_block(
-                inner_v, bmat_v, cmat_v, step_v, decay_v, skip_v, seg_here, cont, zeros_state
-            )
-            flow_v = inflow(step_v, decay_v, seg_here, cont)
-            result_v = part_v + jnp.einsum("th,tn,hpn->thp", flow_v, cmat_v, entry, precision=HIGH)
-            return (result_v, flow_v[-1][:, None, None] * entry + produced_v)
-
-        _, ssd_pull = jax.vjp(
-            mixer_local, inner, bmat, cmat, step, decay, skip_gain[layer], incoming
-        )
-        g_inner, g_bmat, g_cmat, g_step, g_decay, skip_grad, _ = ssd_pull((d_mixed3, carried))
-        g_state = tp_sum(jnp.concatenate([g_bmat, g_cmat], 1).astype(bf), 4).astype(jnp.float32)
+        g_inner, g_both, g_step, g_decay, skip_grad = scan_backward(
+            parts + (decay[None], d_mixed, mixed, incoming, carried)
+        )
+        g_decay = g_decay[0]
+        skip_grad = jnp.sum(skip_grad.reshape(heads_local, head_size), 1)
+        g_state = tp_sum(g_both.astype(bf), 4).astype(jnp.float32)
         g_act = jnp.concatenate([g_inner.reshape(length, inner_local), g_state], 1)
         g_padded, kernel_grad, offset_grad = conv_pull(g_act)
         returned = passed_along(g_padded[: taps - 1], "ctx", -1)
@@ -921,7 +1051,7 @@
     length, rows, cols = args[0].shape[0], args[4].shape[1], args[4].shape[2]
     heads, states = args[7].shape[2], args[6].shape[2]
     fits = ny == 2 and nz <= 4 and n > 1 and rows % 16 == 0 and cols % 128 == 0
-    fits = fits and length % (16 * n) == 0 and length % 128 == 0 and cols >= states + heads
+    fits = fits and length % (16 * n) == 0 and length == SPAN and cols >= states + heads
     return (body_kernels if fits else body)(*args)
 
 

time: 370 us -> 350 us (0.946)
  matrix products: 47.7 us -> 27 us
  local copies, waits for them, and re-layouts: 52.9 us -> 35.3 us
  Pallas kernels: 198 us -> 215 us
    dot_general x28 -> x4, matrix products: 24 us -> 4.89 us  [contract_high(): lax.dot_general(left, right, (((left_dim,), (right_dim,)), ((), ())), pre...]
    pallas_call x0 -> x4, Pallas kernels: none -> 17.8 us  [the longest x2 11.4 us: scan_backward(): pl.pallas_call(back_kernel, out_shape=(f32(length, width), f32(length, 2...]
    convert_element_type x4 -> x11, other arithmetic: 3.17 us -> 11.7 us  [the longest x4 5.49 us: body_kernels(): incoming = passed_along(produced.astype(bf), 'ctx', 1).astype(jnp.float32)]
    mul x23 -> x0, local copies, waits for them, and re-layouts: 8.2 us -> none  [the longest x6 3.51 us: advance(): into[:, :, None] * jnp.einsum('tn,hpn->thp', part_c, carry, precision=HIGH)]
    reduce_sum x6 -> x0, local copies, waits for them, and re-layouts: 4.45 us -> none  [the longest x2 2.15 us: advance(): gap = logs[:, None, :] - logs[None, :, :]]
    another operation x10 -> x5, other arithmetic: 5.16 us -> 0.97 us  [the longest x2 0.73 us: body_kernels(): jnp.stack([seg_here.astype(jnp.float32), (jnp.cumsum(fresh) == 0.0).astyp...]
    unnamed x317 -> x183, local copies, waits for them, and re-layouts: 9.01 us -> 6.62 us
  transfers between devices with their start and end apart: 8 -> 8, of which waited for: 4 -> 5; matrix products, arithmetic and copies ran while one was open for 10% -> 6% of each run, Pallas kernels for 0% -> 0%
where the time goes in v2:
time: 350 us; the launch traced here: 348 us
  Pallas kernels  215 us (61%)
  other arithmetic  37.2 us (11%)
  local copies, waits for them, and re-layouts  35.3 us (10%)
  matrix products  27 us (8%)
  starting transfers between devices  17.2 us (5%)
  waiting for transfers between devices  12.5 us (4%)
  between operations  3.57 us (1%)
    pallas_call x1, Pallas kernels, reduce_grads(): pl.pallas_call(functools.partial(grads_kernel, nz, layers), out_shape=tup...  72 us
    pallas_call x1, Pallas kernels, gather_weights(): pl.pallas_call(functools.partial(weights_kernel, nz, ny), out_shape=(jax....  69.3 us
    pallas_call x6, Pallas kernels, tp_sum(): pl.pallas_call(functools.partial(sum_kernel, n, tallied), out_shape=shape...  56.1 us
    ppermute x8, starting transfers between devices, passed_along(): return lax.ppermute(block, axis, route)  17.2 us
    ppermute x8, waiting for transfers between devices, passed_along(): return lax.ppermute(block, axis, route)  12.5 us
    pallas_call x2, Pallas kernels, scan_backward(): pl.pallas_call(back_kernel, out_shape=(f32(length, width), f32(length, 2...  11.4 us
    dot_general x4, matrix products, contract_cols(): lax.dot_general(left, right, (((1,), (1,)), ((), ())), preferred_element_...  8.78 us
  transfers between devices with their start and end apart: 8, of which 5 were waited for; matrix products, arithmetic and copies ran while one was open for 6% of the time, Pallas kernels for 0%

profile of v2, /device:TPU:0, one launch (start us, length us, event | category | flops | bytes accessed | tf_op | source)
XLA Modules:
  0.0 348.0 jit_solution(3826762389962999598)
XLA Ops:
  0.6 0.8 copy.65
  1.5 1.0 multiply_reduce_fusion.3
  3.4 1.6 maximum_maximum_fusion.refs_2_
  5.0 69.3 %weights.1 = (bf16[2,768,1152]{2,1,0:T(8,128)(2,1)}, bf16[2,768,384]{2,1,0:T(8,128)(2,1)}) custom-call(bf16[2,96,384]{2,1,0:T(8,128)(2,1)} %refs_0_.1, bf16[2,96,384]{2,1,0:T(8,128)(2,1)} %refs_1_.1, bf16[2,96,384]{2,1,0:T(8,128)(2,1)} %maximum_maximum_fusion.refs_2_, bf16[2,96,384]{2,1,0:T(8,128)(2,1)} %refs_3_.1), custom_call_target="tpu_custom_call" | custom-call | tf_op jit(solution)/shard_map/weights/pallas_call | solution.py:242
  74.4 2.1 fusion.97
  76.5 1.5 collective-permute-start
  89.1 3.2 scan_forward.2
  92.3 1.6 convert_element_type.190
  93.9 1.3 collective-permute-start.1
  95.2 0.9 copy.70
  96.3 1.4 collective-permute-done.1
  97.7 1.9 multiply_reduce_fusion.15
  99.6 1.0 convolution_convert_fusion.5.refs_0_
  101.2 10.5 %tpsum.6 = (bf16[128,768]{1,0:T(8,128)(2,1)}, f32[8,128]{1,0:T(8,128)}) custom-call(bf16[128,768]{1,0:T(8,128)(2,1)} %convolution_convert_fusion.5.refs_0_, f32[8,128]{1,0:T(8,128)} %broadcast_in_dim.26.refs_1_), custom_call_target="tpu_custom_call" | custom-call | tf_op jit(solution)/shard_map/tpsum/pallas_call | solution.py:447
  112.4 1.2 multiply_reduce_fusion.2
  113.6 1.9 fusion.98
  115.6 4.2 %collective-permute-start.2 = (bf16[3,640]{1,0:T(4,128)(2,1)S(1)}, bf16[3,640]{1,0:T(4,128)(2,1)S(1)}, u32[]{:S(2)}, u32[]{:S(2)}) collective-permute-start(bf16[3,640]{1,0:T(4,128)(2,1)S(1)} %slice.462), channel_id=1, source_target_pairs={{0,4},{1,5},{2,6},{3,7},{8,12},{9,13},{10,14},{11,15},{16,20},{17,... | collective-permute-start | bytes 11528 | tf_op jit(solution)/shard_map/ppermute | solution.py:20
  123.0 3.2 scan_forward.3
  126.2 1.6 convert_element_type.196
  127.8 4.7 %collective-permute-start.3 = (bf16[384,128]{1,0:T(8,128)(2,1)}, bf16[384,128]{1,0:T(8,128)(2,1)}, u32[]{:S(2)}, u32[]{:S(2)}) collective-permute-start(bf16[384,128]{1,0:T(8,128)(2,1)} %convert_element_type.196), channel_id=1, source_target_pairs={{0,4},{1,5},{2,6},{3,7},{8,12},{9,13},{10,14},{11,15},{16,20},{17,... | collective-permute-start | bytes 294920 | tf_op jit(solution)/shard_map/ppermute | solution.py:20
  134.0 0.9 copy.74
  135.0 2.0 multiply_reduce_fusion.14
  137.1 2.1 convolution_convert_fusion.4.refs_0_
  139.8 9.5 %tpsum.7 = (bf16[128,768]{1,0:T(8,128)(2,1)}, f32[8,128]{1,0:T(8,128)}) custom-call(bf16[128,768]{1,0:T(8,128)(2,1)} %convolution_convert_fusion.4.refs_0_, f32[8,128]{1,0:T(8,128)} %broadcast_in_dim.29.refs_1_), custom_call_target="tpu_custom_call" | custom-call | tf_op jit(solution)/shard_map/tpsum/pallas_call | solution.py:447
  150.1 1.1 multiply_reduce_fusion.1
  151.9 1.7 multiply_multiply_fusion.7
  154.0 1.5 collective-permute-start.4
  155.6 1.2 fusion.12.refs_3_
  158.1 1.6 convert_element_type.203.enter_ref
  159.7 1.5 collective-permute-done.4
  161.9 5.7 %scan_backward.2 = (f32[128,384]{1,0:T(8,128)}, f32[128,256]{1,0:T(8,128)}, f32[128,6]{1,0:T(8,128)}, f32[1,6]{1,0:T(1,128)}, f32[1,384]{1,0:T(1,128)}) custom-call(f32[128,384]{1,0:T(8,128)} %slice.472.x_ref, f32[128,256]{1,0:T(8,128)} %slice.473.bc_ref, f32[128,6]{1,0:T(8,128)} %get-tuple-element.157.step_ref, f32[128,6]{1,0:T(8,128)} %copy-done.5, ...), custom_call_target="tpu_custom_call" | custom-call | tf_op jit(solution)/shard_map/scan_backward/pallas_call | solution.py:562
  167.7 1.5 convert_element_type.206.refs_0_
  169.2 8.5 %tpsum.8 = bf16[128,256]{1,0:T(8,128)(2,1)} custom-call(bf16[128,256]{1,0:T(8,128)(2,1)} %convert_element_type.206.refs_0_), custom_call_target="tpu_custom_call" | custom-call | tf_op jit(solution)/shard_map/tpsum/pallas_call | solution.py:447
  177.7 0.9 convert_element_type.207
  178.6 1.3 multiply_reduce_fusion.7
  181.0 1.5 fusion.89
  182.4 1.3 collective-permute-start.5
  185.7 2.3 collective-permute-done.5
  188.3 2.8 fusion.16.refs_0_
  191.2 9.5 %tpsum.9 = bf16[128,768]{1,0:T(8,128)(2,1)} custom-call(bf16[128,768]{1,0:T(8,128)(2,1)} %fusion.16.refs_0_), custom_call_target="tpu_custom_call" | custom-call | tf_op jit(solution)/shard_map/tpsum/pallas_call | solution.py:447
  200.7 1.2 fusion.35
  202.0 1.2 fusion.34
  203.9 1.2 convolution_convert_fusion.3.refs_1_
  205.1 1.3 multiply_multiply_fusion.6
  207.0 1.5 collective-permute-start.6
  208.5 1.9 convolution_convert_fusion.refs_2_
  210.5 3.5 %collective-permute-done.6 = bf16[384,128]{1,0:T(8,128)(2,1)S(1)} collective-permute-done((bf16[384,128]{1,0:T(8,128)(2,1)S(1)}, bf16[384,128]{1,0:T(8,128)(2,1)S(1)}, u32[]{:S(2)}, u32[]{:S(2)}) %collective-permute-start.6) | collective-permute-done | bytes 98336 | tf_op jit(solution)/shard_map/ppermute | solution.py:20
  214.8 5.7 %scan_backward.3 = (f32[128,384]{1,0:T(8,128)}, f32[128,256]{1,0:T(8,128)}, f32[128,6]{1,0:T(8,128)}, f32[1,6]{1,0:T(1,128)}, f32[1,384]{1,0:T(1,128)}) custom-call(f32[128,384]{1,0:T(8,128)} %slice.455.x_ref, f32[128,256]{1,0:T(8,128)} %slice.456.bc_ref, f32[128,6]{1,0:T(8,128)} %get-tuple-element.165.step_ref, f32[128,6]{1,0:T(8,128)} %copy-done.4, ...), custom_call_target="tpu_custom_call" | custom-call | tf_op jit(solution)/shard_map/scan_backward/pallas_call | solution.py:562
  220.5 1.6 convert_element_type.218.refs_0_
  222.1 8.5 %tpsum.10 = bf16[128,256]{1,0:T(8,128)(2,1)} custom-call(bf16[128,256]{1,0:T(8,128)(2,1)} %convert_element_type.218.refs_0_), custom_call_target="tpu_custom_call" | custom-call | tf_op jit(solution)/shard_map/tpsum/pallas_call | solution.py:447
  230.6 0.9 convert_element_type.219
  231.5 1.3 multiply_reduce_fusion.11
  234.0 0.9 fusion.88
  234.9 1.3 collective-permute-start.7
  236.7 3.8 %collective-permute-done.7 = f32[3,640]{1,0:T(4,128)S(1)} collective-permute-done((f32[3,640]{1,0:T(4,128)S(1)}, f32[3,640]{1,0:T(4,128)S(1)}, u32[]{:S(2)}, u32[]{:S(2)}) %collective-permute-start.7) | collective-permute-done | bytes 7712 | tf_op jit(solution)/shard_map/ppermute | solution.py:20
  240.8 2.8 fusion.13.refs_0_
  243.6 9.5 %tpsum.11 = bf16[128,768]{1,0:T(8,128)(2,1)} custom-call(bf16[128,768]{1,0:T(8,128)(2,1)} %fusion.13.refs_0_), custom_call_target="tpu_custom_call" | custom-call | tf_op jit(solution)/shard_map/tpsum/pallas_call | solution.py:447
  253.0 1.1 fusion.36
  254.3 2.0 convolution_convert_fusion.1.refs_0_
  257.0 72.0 %grads.1 = (f32[2,96,384]{2,1,0:T(8,128)}, f32[2,96,384]{2,1,0:T(8,128)}, f32[2,96,384]{2,1,0:T(8,128)}, f32[2,96,384]{2,1,0:T(8,128)}, f32[64,128]{1,0:T(8,128)}) custom-call(bf16[768,1152]{1,0:T(8,128)(2,1)} %convolution_convert_fusion.1.refs_0_, bf16[768,384]{1,0:T(8,128)(2,1)} %convolution_convert_fusion.3.refs_1_, ...), custom_call_target="tpu_custom_call" | custom-call | tf_op jit(solution)/shard_map/grads/pallas_call | solution.py:361
  329.1 1.7 slice.431
  330.8 0.9 slice.432
  335.9 0.9 fusion.94
  343.1 1.3 fusion.48
  (334 shorter events, 43.2 us)
Async XLA Ops:
  2.5 74.0 %copy-start.81 = (f32[128]{0:T(128)}, f32[128]{0:T(128)S(1)}, u32[]{:S(2)}) copy-start(f32[128]{0:T(128)S(1)} %multiply_reduce_fusion.3) | copy-start | bytes 1540
  2.5 74.0 %copy-start.51 = (f32[128]{0:T(128)}, f32[128]{0:T(128)S(1)}, u32[]{:S(2)}) copy-start(f32[128]{0:T(128)S(1)} %fusion.78) | copy-start | bytes 1540
  5.0 73.0 %copy-start.78 = (s32[1,256]{1,0:T(1,128)S(1)}, s32[1,256]{1,0:T(1,128)}, u32[]{:S(2)}) copy-start(s32[1,256]{1,0:T(1,128)} %param.18) | copy-start | bytes 3076
  5.0 75.1 %copy-start.50 = (f32[2,4,384]{2,1,0:T(4,128)S(1)}, f32[2,4,384]{2,1,0:T(4,128)}, u32[]{:S(2)}) copy-start(f32[2,4,384]{2,1,0:T(4,128)} %param.25) | copy-start | bytes 36868
  5.0 75.1 %copy-start.53 = (f32[2,4,256]{2,1,0:T(4,128)S(1)}, f32[2,4,256]{2,1,0:T(4,128)}, u32[]{:S(2)}) copy-start(f32[2,4,256]{2,1,0:T(4,128)} %param.27) | copy-start | bytes 24580
  5.0 75.1 %copy-start.66 = (f32[2,384]{1,0:T(2,128)S(1)}, f32[2,384]{1,0:T(2,128)}, u32[]{:S(2)}) copy-start(f32[2,384]{1,0:T(2,128)} %param.26) | copy-start | bytes 9220
  5.0 75.1 %copy-start.74 = (f32[2,256]{1,0:T(2,128)S(1)}, f32[2,256]{1,0:T(2,128)}, u32[]{:S(2)}) copy-start(f32[2,256]{1,0:T(2,128)} %param.28) | copy-start | bytes 6148
  74.3 8.1 %copy-start.62 = (f32[2,6]{1,0:T(2,128)S(1)}, f32[2,6]{1,0:T(2,128)}, u32[]{:S(2)}) copy-start(f32[2,6]{1,0:T(2,128)} %param.30) | copy-start | bytes 148
  74.4 8.7 %copy-start.79 = (f32[2,6]{1,0:T(2,128)S(1)}, f32[2,6]{1,0:T(2,128)}, u32[]{:S(2)}) copy-start(f32[2,6]{1,0:T(2,128)} %param.29) | copy-start | bytes 148
  74.4 9.3 %copy-start.80 = (f32[2,6]{1,0:T(2,128)S(1)}, f32[2,6]{1,0:T(2,128)}, u32[]{:S(2)}) copy-start(f32[2,6]{1,0:T(2,128)} %param.31) | copy-start | bytes 148
  74.4 9.3 %copy-start.67 = (f32[2,384]{1,0:T(2,128)S(1)}, f32[2,384]{1,0:T(2,128)}, u32[]{:S(2)}) copy-start(f32[2,384]{1,0:T(2,128)} %param.32) | copy-start | bytes 9220
  76.5 21.2 %copy-start.7 = (f32[128,1152]{1,0:T(8,128)}, f32[128,1152]{1,0:T(8,128)S(1)}, u32[]{:S(2)}) copy-start(f32[128,1152]{1,0:T(8,128)S(1)} %get-tuple-element.212) | copy-start | bytes 1769476
  76.5 10.8 %collective-permute-start = (bf16[3,640]{1,0:T(4,128)(2,1)S(1)}, bf16[3,640]{1,0:T(4,128)(2,1)S(1)}, u32[]{:S(2)}, u32[]{:S(2)}) collective-permute-start(bf16[3,640]{1,0:T(4,128)(2,1)S(1)} %slice.445), channel_id=1, source_target_pairs={{0,4},{1,5},{2,6},{3,7},{8,12},{9,13},{10,14},{11,15},{16,20},{17,... | collective-permute-start | bytes 11528 | tf_op jit(solution)/shard_map/ppermute | solution.py:20
  80.1 41.2 %copy-start.31 = (f32[128]{0:T(128)}, f32[128]{0:T(128)S(1)}, u32[]{:S(2)}) copy-start(f32[128]{0:T(128)S(1)} %get-tuple-element.208) | copy-start | bytes 1540
  80.1 41.2 %copy-start.34 = (f32[128]{0:T(128)}, f32[128]{0:T(128)S(1)}, u32[]{:S(2)}) copy-start(f32[128]{0:T(128)S(1)} %get-tuple-element.209) | copy-start | bytes 1540
  80.1 41.2 %copy-start.37 = (f32[128]{0:T(128)}, f32[128]{0:T(128)S(1)}, u32[]{:S(2)}) copy-start(f32[128]{0:T(128)S(1)} %get-tuple-element.210) | copy-start | bytes 1540
  83.7 15.9 %copy-start.46 = (f32[384]{0:T(512)}, f32[384]{0:T(512)S(1)}, u32[]{:S(2)}) copy-start(f32[384]{0:T(512)S(1)} %get-tuple-element.143) | copy-start | bytes 4612
  83.7 53.4 %copy-start.48 = (f32[384]{0:T(512)}, f32[384]{0:T(512)S(1)}, u32[]{:S(2)}) copy-start(f32[384]{0:T(512)S(1)} %get-tuple-element.142) | copy-start | bytes 4612
  87.3 34.0 %copy-start.24 = (f32[640]{0:T(1024)}, f32[640]{0:T(1024)S(1)}, u32[]{:S(2)}) copy-start(f32[640]{0:T(1024)S(1)} %get-tuple-element.133) | copy-start | bytes 7684
  87.3 34.0 %copy-start.26 = (f32[640]{0:T(1024)}, f32[640]{0:T(1024)S(1)}, u32[]{:S(2)}) copy-start(f32[640]{0:T(1024)S(1)} %get-tuple-element.134) | copy-start | bytes 7684
  87.3 34.0 %copy-start.28 = (f32[640]{0:T(1024)}, f32[640]{0:T(1024)S(1)}, u32[]{:S(2)}) copy-start(f32[640]{0:T(1024)S(1)} %get-tuple-element.135) | copy-start | bytes 7684
  87.4 7.8 %copy-start.64 = (f32[1,256]{1,0:T(1,128)S(1)}, f32[1,256]{1,0:T(1,128)}, u32[]{:S(2)}) copy-start(f32[1,256]{1,0:T(1,128)} %get-tuple-element.190) | copy-start | bytes 3076
  87.7 11.8 %copy-start.2 = (bf16[2,768,384]{2,1,0:T(8,128)(2,1)S(1)}, bf16[2,768,384]{2,1,0:T(8,128)(2,1)}, u32[]{:S(2)}) copy-start(bf16[2,768,384]{2,1,0:T(8,128)(2,1)} %get-tuple-element.47) | copy-start | bytes 3538948
  92.3 20.1 %copy-start = (bf16[128,768]{1,0:T(8,128)(2,1)S(1)}, bf16[128,768]{1,0:T(8,128)(2,1)}, u32[]{:S(2)}) copy-start(bf16[128,768]{1,0:T(8,128)(2,1)} %param.17) | copy-start | bytes 589828
  93.9 3.8 %collective-permute-start.1 = (bf16[384,128]{1,0:T(8,128)(2,1)}, bf16[384,128]{1,0:T(8,128)(2,1)S(1)}, u32[]{:S(2)}, u32[]{:S(2)}) collective-permute-start(bf16[384,128]{1,0:T(8,128)(2,1)} %convert_element_type.190), channel_id=1, source_target_pairs={{0,4},{1,5},{2,6},{3,7},{8,12},{9,13},{10,14},{11,15},{16,20},{17,... | collective-permute-start | bytes 294920 | tf_op jit(solution)/shard_map/ppermute | solution.py:20
  96.3 16.1 %copy-start.10 = (f32[128,384]{1,0:T(8,128)}, f32[128,384]{1,0:T(8,128)S(1)}, u32[]{:S(2)}) copy-start(f32[128,384]{1,0:T(8,128)S(1)} %copy.71) | copy-start | bytes 589828
  99.6 12.8 %copy-start.14 = (f32[128,384]{1,0:T(8,128)}, f32[128,384]{1,0:T(8,128)S(1)}, u32[]{:S(2)}) copy-start(f32[128,384]{1,0:T(8,128)S(1)} %get-tuple-element.163) | copy-start | bytes 589828
  112.4 7.4 %copy-start.60 = (f32[6]{0:T(128)S(1)}, f32[6]{0:T(128)}, u32[]{:S(2)}) copy-start(f32[6]{0:T(128)} %get-tuple-element.200) | copy-start | bytes 76
  115.6 5.6 %collective-permute-start.2 = (bf16[3,640]{1,0:T(4,128)(2,1)S(1)}, bf16[3,640]{1,0:T(4,128)(2,1)S(1)}, u32[]{:S(2)}, u32[]{:S(2)}) collective-permute-start(bf16[3,640]{1,0:T(4,128)(2,1)S(1)} %slice.462), channel_id=1, source_target_pairs={{0,4},{1,5},{2,6},{3,7},{8,12},{9,13},{10,14},{11,15},{16,20},{17,... | collective-permute-start | bytes 11528 | tf_op jit(solution)/shard_map/ppermute | solution.py:20
  127.8 7.3 %collective-permute-start.3 = (bf16[384,128]{1,0:T(8,128)(2,1)}, bf16[384,128]{1,0:T(8,128)(2,1)}, u32[]{:S(2)}, u32[]{:S(2)}) collective-permute-start(bf16[384,128]{1,0:T(8,128)(2,1)} %convert_element_type.196), channel_id=1, source_target_pairs={{0,4},{1,5},{2,6},{3,7},{8,12},{9,13},{10,14},{11,15},{16,20},{17,... | collective-permute-start | bytes 294920 | tf_op jit(solution)/shard_map/ppermute | solution.py:20
  133.2 16.8 %copy-start.1 = (f32[128,768]{1,0:T(8,128)S(1)}, f32[128,768]{1,0:T(8,128)}, u32[]{:S(2)}) copy-start(f32[128,768]{1,0:T(8,128)} %param.19) | copy-start | bytes 1179652
  137.1 14.8 %copy-start.16 = (f32[128,384]{1,0:T(8,128)}, f32[128,384]{1,0:T(8,128)S(1)}, u32[]{:S(2)}) copy-start(f32[128,384]{1,0:T(8,128)S(1)} %get-tuple-element.155) | copy-start | bytes 589828
  153.5 8.4 %copy-start.9 = (f32[128,384]{1,0:T(8,128)}, f32[128,384]{1,0:T(8,128)S(1)}, u32[]{:S(2)}) copy-start(f32[128,384]{1,0:T(8,128)S(1)} %get-tuple-element.170.dm_ref) | copy-start | bytes 589828
  154.0 7.2 %collective-permute-start.4 = (bf16[384,128]{1,0:T(8,128)(2,1)S(1)}, bf16[384,128]{1,0:T(8,128)(2,1)S(1)}, u32[]{:S(2)}, u32[]{:S(2)}) collective-permute-start(bf16[384,128]{1,0:T(8,128)(2,1)S(1)} %convolution_convert_fusion.7), channel_id=1, source_target_pairs={{4,0},{5,1},{6,2},{7,3},{12,8},{13,9},{14,10},{15,11},{20,16},{21,... | collective-permute-start | bytes 294920 | tf_op jit(solution)/shard_map/ppermute | solution.py:20
  156.8 21.8 %copy-start.32 = (f32[128]{0:T(128)S(1)}, f32[128]{0:T(128)}, u32[]{:S(2)}) copy-start(f32[128]{0:T(128)} %copy-done.31) | copy-start | bytes 1540
  156.8 21.8 %copy-start.35 = (f32[128]{0:T(128)S(1)}, f32[128]{0:T(128)}, u32[]{:S(2)}) copy-start(f32[128]{0:T(128)} %copy-done.34) | copy-start | bytes 1540
  156.8 21.8 %copy-start.38 = (f32[128]{0:T(128)S(1)}, f32[128]{0:T(128)}, u32[]{:S(2)}) copy-start(f32[128]{0:T(128)} %copy-done.37) | copy-start | bytes 1540
  161.9 18.0 %copy-start.25 = (f32[640]{0:T(1024)S(1)}, f32[640]{0:T(1024)}, u32[]{:S(2)}) copy-start(f32[640]{0:T(1024)} %copy-done.24) | copy-start | bytes 7684
  161.9 18.0 %copy-start.27 = (f32[640]{0:T(1024)S(1)}, f32[640]{0:T(1024)}, u32[]{:S(2)}) copy-start(f32[640]{0:T(1024)} %copy-done.26) | copy-start | bytes 7684
  161.9 18.0 %copy-start.29 = (f32[640]{0:T(1024)S(1)}, f32[640]{0:T(1024)}, u32[]{:S(2)}) copy-start(f32[640]{0:T(1024)} %copy-done.28) | copy-start | bytes 7684
  182.4 5.6 %collective-permute-start.5 = (f32[3,640]{1,0:T(4,128)S(1)}, f32[3,640]{1,0:T(4,128)S(1)}, u32[]{:S(2)}, u32[]{:S(2)}) collective-permute-start(f32[3,640]{1,0:T(4,128)S(1)} %pad_add_fusion.3), channel_id=1, source_target_pairs={{4,0},{5,1},{6,2},{7,3},{12,8},{13,9},{14,10},{15,11},{20,16},{21,... | collective-permute-start | bytes 23048 | tf_op jit(solution)/shard_map/ppermute | solution.py:20
  183.7 7.4 %copy-start.40 = (f32[1,640]{1,0:T(1,128)}, f32[1,640]{1,0:T(1,128)S(1)}, u32[]{:S(2)}) copy-start(f32[1,640]{1,0:T(1,128)S(1)} %reshape.293) | copy-start | bytes 7684
  183.8 7.4 %copy-start.42 = (f32[1,640]{1,0:T(1,128)}, f32[1,640]{1,0:T(1,128)S(1)}, u32[]{:S(2)}) copy-start(f32[1,640]{1,0:T(1,128)S(1)} %reshape.294) | copy-start | bytes 7684
  188.2 12.5 %copy-start.55 = (f32[128]{0:T(128)S(1)}, f32[128]{0:T(128)}, u32[]{:S(2)}) copy-start(f32[128]{0:T(128)} %copy-done.54) | copy-start | bytes 1540
  188.3 13.6 %copy-start.84 = (f32[128]{0:T(128)S(1)}, f32[128]{0:T(128)}, u32[]{:S(2)}) copy-start(f32[128]{0:T(128)} %copy-done.83) | copy-start | bytes 1540
  188.3 13.6 %copy-start.12 = (bf16[128,768]{1,0:T(8,128)(2,1)S(1)}, bf16[128,768]{1,0:T(8,128)(2,1)}, u32[]{:S(2)}) copy-start(bf16[128,768]{1,0:T(8,128)(2,1)} %get-tuple-element.48) | copy-start | bytes 589828
  191.2 12.7 %copy-start.15 = (f32[128,384]{1,0:T(8,128)S(1)}, f32[128,384]{1,0:T(8,128)}, u32[]{:S(2)}) copy-start(f32[128,384]{1,0:T(8,128)} %copy-done.14) | copy-start | bytes 589828
  191.2 12.7 %copy-start.47 = (f32[384]{0:T(512)S(1)}, f32[384]{0:T(512)}, u32[]{:S(2)}) copy-start(f32[384]{0:T(512)} %copy-done.46) | copy-start | bytes 4612
  191.2 12.7 %copy-start.71 = (f32[128]{0:T(128)S(1)}, f32[128]{0:T(128)}, u32[]{:S(2)}) copy-start(f32[128]{0:T(128)} %copy-done.70) | copy-start | bytes 1540
  206.4 8.4 %copy-start.8 = (f32[128,384]{1,0:T(8,128)}, f32[128,384]{1,0:T(8,128)S(1)}, u32[]{:S(2)}) copy-start(f32[128,384]{1,0:T(8,128)S(1)} %get-tuple-element.168.dm_ref) | copy-start | bytes 589828
  206.9 24.5 %copy-start.33 = (f32[128]{0:T(128)S(1)}, f32[128]{0:T(128)}, u32[]{:S(2)}) copy-start(f32[128]{0:T(128)} %copy-done.31) | copy-start | bytes 1540
  206.9 24.5 %copy-start.36 = (f32[128]{0:T(128)S(1)}, f32[128]{0:T(128)}, u32[]{:S(2)}) copy-start(f32[128]{0:T(128)} %copy-done.34) | copy-start | bytes 1540
  207.0 24.5 %copy-start.39 = (f32[128]{0:T(128)S(1)}, f32[128]{0:T(128)}, u32[]{:S(2)}) copy-start(f32[128]{0:T(128)} %copy-done.37) | copy-start | bytes 1540
  207.0 7.1 %collective-permute-start.6 = (bf16[384,128]{1,0:T(8,128)(2,1)S(1)}, bf16[384,128]{1,0:T(8,128)(2,1)S(1)}, u32[]{:S(2)}, u32[]{:S(2)}) collective-permute-start(bf16[384,128]{1,0:T(8,128)(2,1)S(1)} %convolution_convert_fusion.6), channel_id=1, source_target_pairs={{4,0},{5,1},{6,2},{7,3},{12,8},{13,9},{14,10},{15,11},{20,16},{21,... | collective-permute-start | bytes 294920 | tf_op jit(solution)/shard_map/ppermute | solution.py:20
  220.5 12.4 %copy-start.41 = (f32[1,640]{1,0:T(1,128)S(1)}, f32[1,640]{1,0:T(1,128)}, u32[]{:S(2)}) copy-start(f32[1,640]{1,0:T(1,128)} %copy-done.40) | copy-start | bytes 7684
  220.5 12.4 %copy-start.43 = (f32[1,640]{1,0:T(1,128)S(1)}, f32[1,640]{1,0:T(1,128)}, u32[]{:S(2)}) copy-start(f32[1,640]{1,0:T(1,128)} %copy-done.42) | copy-start | bytes 7684
  220.5 12.4 %copy-start.45 = (f32[1,640]{1,0:T(1,128)S(1)}, f32[1,640]{1,0:T(1,128)}, u32[]{:S(2)}) copy-start(f32[1,640]{1,0:T(1,128)} %copy-done.44) | copy-start | bytes 7684
  234.9 5.6 %collective-permute-start.7 = (f32[3,640]{1,0:T(4,128)S(1)}, f32[3,640]{1,0:T(4,128)S(1)}, u32[]{:S(2)}, u32[]{:S(2)}) collective-permute-start(f32[3,640]{1,0:T(4,128)S(1)} %pad_add_fusion.2), channel_id=1, source_target_pairs={{4,0},{5,1},{6,2},{7,3},{12,8},{13,9},{14,10},{15,11},{20,16},{21,... | collective-permute-start | bytes 23048 | tf_op jit(solution)/shard_map/ppermute | solution.py:20
  240.7 12.4 %copy-start.52 = (f32[128]{0:T(128)S(1)}, f32[128]{0:T(128)}, u32[]{:S(2)}) copy-start(f32[128]{0:T(128)} %copy-done.51) | copy-start | bytes 1540
  257.0 86.0 %copy-start.82 = (f32[128]{0:T(128)S(1)}, f32[128]{0:T(128)}, u32[]{:S(2)}) copy-start(f32[128]{0:T(128)} %copy-done.81) | copy-start | bytes 1540
  257.0 86.0 %copy-start.69 = (f32[128]{0:T(128)S(1)}, f32[128]{0:T(128)}, u32[]{:S(2)}) copy-start(f32[128]{0:T(128)} %copy-done.68) | copy-start | bytes 1540
  329.1 16.8 %copy-start.20 = (f32[2,96,384]{2,1,0:T(8,128)S(1)}, f32[2,96,384]{2,1,0:T(8,128)}, u32[]{:S(2)}) copy-start(f32[2,96,384]{2,1,0:T(8,128)} %get-tuple-element.246) | copy-start | bytes 884740
  329.1 17.5 %copy-start.19 = (f32[2,96,384]{2,1,0:T(8,128)S(1)}, f32[2,96,384]{2,1,0:T(8,128)}, u32[]{:S(2)}) copy-start(f32[2,96,384]{2,1,0:T(8,128)} %get-tuple-element.247) | copy-start | bytes 884740
  329.1 18.2 %copy-start.18 = (f32[2,96,384]{2,1,0:T(8,128)S(1)}, f32[2,96,384]{2,1,0:T(8,128)}, u32[]{:S(2)}) copy-start(f32[2,96,384]{2,1,0:T(8,128)} %get-tuple-element.258) | copy-start | bytes 884740
  (32 other events, 118.0 us)

commit v3 on v2

--- a/solution.py
+++ b/solution.py
@@ -263,10 +263,15 @@
     ins = refs[: 2 * layers]
     small = refs[2 * layers]
     outs = refs[2 * layers + 1 : 2 * layers + 5]
-    small_out = refs[2 * layers + 5]
-    rest = refs[2 * layers + 6 :]
+    step_out = refs[2 * layers + 5]
+    small_outs = refs[2 * layers + 6 : 2 * layers + 15]
+    rest = refs[2 * layers + 15 :]
+    extra, = rest[-1:]
+    wide, heads = outs[2].shape[2], step_out.shape[2]
+    outs = (outs[0], outs[1], extra, outs[3])
+    state_out = refs[2 * layers + 3]
     yin, ymix, pin, pmix, zin, zmix, srecv = rest[:7]
-    ysend, yrecv, zsend, zrecv, ssend, srec, sown = rest[7:]
+    ysend, yrecv, zsend, zrecv, ssend, srec, sown = rest[7:-1]
     ny = 2
     z, y = lax.axis_index("fsdp"), lax.axis_index("ctx")
     other = 1 - y
@@ -341,18 +346,29 @@
         for d in range(1, nz):
             total = total + zmix[layer, d - 1].astype(jnp.float32)
         outs[3][layer] = total
+    state_out[...] = extra[:, :, :wide]
+    step_out[...] = extra[:, :, wide : wide + heads]
     keep.wait()
     for copy in scopies:
         copy.wait_recv()
     total = srecv[0]
     for i in range(1, nz * ny):
         total = total + srecv[i]
-    small_out[...] = total
+    start = 0
+    for out in small_outs:
+        width = out.shape[-1]
+        if len(out.shape) == 2:
+            out[...] = total[start : start + layers, :width]
+            start += layers
+        else:
+            for layer in range(layers):
+                out[layer] = total[start : start + out.shape[1], :width]
+                start += out.shape[1]
     for copy in list(ycopies.values()) + list(zcopies.values()) + scopies:
         copy.wait_send()
 
 
-def reduce_grads(grads, small):
+def reduce_grads(grads, small, shapes, wide, heads):
     nz = lax.axis_size("fsdp")
     layers = len(grads) // 2
     full, cols = grads[1].shape
@@ -360,10 +376,12 @@
     dma, bf = pltpu.SemaphoreType.DMA, jnp.bfloat16
     return pl.pallas_call(
         functools.partial(grads_kernel, nz, layers),
-        out_shape=tuple(jax.ShapeDtypeStruct((layers, rows, cols), jnp.float32) for _ in range(4))
-        + (jax.ShapeDtypeStruct(small.shape, jnp.float32),),
+        out_shape=tuple(
+            jax.ShapeDtypeStruct(shape, jnp.float32)
+            for shape in [(layers, rows, width) for width in (cols, cols, wide, cols, heads)] + shapes
+        ),
         in_specs=[VM] * (2 * layers + 1),
-        out_specs=(VM,) * 5,
+        out_specs=(VM,) * (5 + len(shapes)),
         scratch_shapes=[
             pltpu.VMEM((layers, nz, rows, 3 * cols), bf),
             pltpu.VMEM((layers, nz, rows, cols), bf),
@@ -379,6 +397,7 @@
             dma((2 * nz - 1,)),
             dma((2 * nz - 1,)),
             dma,
+            pltpu.VMEM((layers, rows, cols), jnp.float32),
         ],
         compiler_params=pltpu.CompilerParams(collective_id=2, has_side_effects=True),
         name="grads",
@@ -432,6 +451,42 @@
         copy.wait_send()
 
 
+def share_kernel(n, x, out, seen, send, recv, own):
+    me = lax.axis_index("tp")
+    peers = [lax.rem(me + d, n) for d in range(1, n)]
+    greet([{"tp": peer} for peer in peers])
+    keep = pltpu.make_async_copy(x, seen.at[me], own)
+    keep.start()
+    copies = []
+    for d, peer in enumerate(peers):
+        copy = remote(x, seen.at[me], send.at[d], recv.at[d], {"tp": peer})
+        copy.start()
+        copies.append(copy)
+    keep.wait()
+    for copy in copies:
+        copy.wait_recv()
+    total = seen[0].astype(jnp.float32)
+    for i in range(1, n):
+        total = total + seen[i].astype(jnp.float32)
+    out[...] = total
+    for copy in copies:
+        copy.wait_send()
+
+
+def share_sum(x, ident):
+    n = lax.axis_size("tp")
+    dma = pltpu.SemaphoreType.DMA
+    return pl.pallas_call(
+        functools.partial(share_kernel, n),
+        out_shape=jax.ShapeDtypeStruct(x.shape, jnp.float32),
+        in_specs=[VM],
+        out_specs=VM,
+        scratch_shapes=[pltpu.VMEM((n,) + x.shape, x.dtype), dma((n - 1,)), dma((n - 1,)), dma],
+        compiler_params=pltpu.CompilerParams(collective_id=ident, has_side_effects=True),
+        name="share",
+    )(x)
+
+
 def tp_sum(x, ident, tally=None):
     n = lax.axis_size("tp")
     rows, cols = x.shape
@@ -496,7 +551,7 @@
         x_ref, bc_ref, step_ref, sd_ref, sdt_ref, aux_ref, row_ref
     )
     into_ref[...] = into
-    made_ref[...] = dots(scaled * rep(tail), bmat, ((0,), (0,)))
+    made_ref[...] = dots(scaled * rep(tail), bmat, ((0,), (0,))).astype(made_ref.dtype)
     for h in range(heads):
         at = slice(h * size, (h + 1) * size)
         local = dots(weights(h) * scores, scaled[:, at], ((1,), (0,)))
@@ -512,7 +567,8 @@
     )
     length, states = bmat.shape
     fold = lambda v: dots(v, spread, ((1,), (1,)))
-    x, dm, enter, leave = x_ref[...], dm_ref[...], enter_ref[...], leave_ref[...]
+    x, dm = x_ref[...], dm_ref[...]
+    enter, leave = enter_ref[...].astype(jnp.float32), leave_ref[...].astype(jnp.float32)
     skip = skip_ref[...]
     tails = rep(tail)
     from_state = tails * dots(bmat, leave, ((1,), (1,)))
@@ -523,12 +579,10 @@
         dm_h = dm_ref[:, at]
         d_scores += weight * dots(dm_h, scaled[:, at], ((1,), (1,)))
         local_ref[:, at] = dots(weight * scores, dm_h, ((0,), (0,)))
-    dbc_ref[:, :states] = dots(scaled * tails, leave, ((1,), (0,))) + dots(
-        d_scores, cmat, ((0,), (0,))
-    )
-    dbc_ref[:, states:] = dots(dm * rep(into), enter, ((1,), (0,))) + dots(
-        d_scores, bmat, ((1,), (0,))
-    )
+    d_b = dots(scaled * tails, leave, ((1,), (0,))) + dots(d_scores, cmat, ((0,), (0,)))
+    d_c = dots(dm * rep(into), enter, ((1,), (0,))) + dots(d_scores, bmat, ((1,), (0,)))
+    dbc_ref[:, :states] = d_b.astype(dbc_ref.dtype)
+    dbc_ref[:, states:] = d_c.astype(dbc_ref.dtype)
     d_scaled = local_ref[...] + from_state
     dx_ref[...] = d_scaled * rep(step_ref[...]) + skip * dm
     d_logs = fold(dm * (mixed_ref[...] - skip * x) - scaled * d_scaled)
@@ -548,7 +602,11 @@
     f32 = lambda *shape: jax.ShapeDtypeStruct(shape, jnp.float32)
     return pl.pallas_call(
         scan_kernel,
-        out_shape=(f32(length, width), f32(width, states), f32(length, heads)),
+        out_shape=(
+            f32(length, width),
+            jax.ShapeDtypeStruct((width, states), jnp.bfloat16),
+            f32(length, heads),
+        ),
         in_specs=[VM] * len(parts),
         out_specs=(VM,) * 3,
         name="scan_forward",
@@ -562,7 +620,9 @@
     return pl.pallas_call(
         back_kernel,
         out_shape=(
-            f32(length, width), f32(length, 2 * states), f32(length, heads), f32(1, heads), f32(1, width),
+            f32(length, width),
+            jax.ShapeDtypeStruct((length, 2 * states), jnp.bfloat16),
+            f32(length, heads), f32(1, heads), f32(1, width),
         ),
         in_specs=[VM] * len(parts),
         out_specs=(VM,) * 5,
@@ -928,8 +988,10 @@
             jnp.repeat(skip_gain[layer], head_size)[None],
         )
         partial_mixed, produced, flow = scan_forward(parts)
-        incoming = passed_along(produced.astype(bf), "ctx", 1).astype(jnp.float32)
-        reach = contract_high(act[:, inner_local + state_size :], incoming, 1, 1)
+        incoming = passed_along(produced, "ctx", 1)
+        reach = contract_high(
+            act[:, inner_local + state_size :], incoming.astype(jnp.float32), 1, 1
+        )
         mixed = partial_mixed + jnp.repeat(flow, head_size, axis=1) * reach
         gated = mixed * jax.nn.silu(gate)
         squares = jnp.broadcast_to(jnp.sum(gated * gated, 1)[None], (8, length))
@@ -969,13 +1031,13 @@
         )
         cmat = parts[1][:, state_size:]
         adjoint = contract_high(jnp.repeat(flow, head_size, axis=1) * d_mixed, cmat, 0, 0)
-        carried = passed_along(adjoint.astype(bf), "ctx", -1).astype(jnp.float32)
+        carried = passed_along(adjoint.astype(bf), "ctx", -1)
         g_inner, g_both, g_step, g_decay, skip_grad = scan_backward(
             parts + (decay[None], d_mixed, mixed, incoming, carried)
         )
         g_decay = g_decay[0]
         skip_grad = jnp.sum(skip_grad.reshape(heads_local, head_size), 1)
-        g_state = tp_sum(g_both.astype(bf), 4).astype(jnp.float32)
+        g_state = share_sum(g_both, 4)
         g_act = jnp.concatenate([g_inner.reshape(length, inner_local), g_state], 1)
         g_padded, kernel_grad, offset_grad = conv_pull(g_act)
         returned = passed_along(g_padded[: taps - 1], "ctx", -1)
@@ -1016,24 +1078,25 @@
         return jnp.stack([groups[layer][member] for layer in range(layers)])
 
     members = [stack_member(small_grads, member) for member in range(9)]
-    flat = jnp.concatenate([m.reshape(-1) for m in members])
-    fill = -flat.shape[0] % 1024
-    flat = jnp.concatenate([flat, jnp.zeros((fill,), jnp.float32)]).reshape(-1, 128)
+    flat = jnp.concatenate(
+        [
+            jnp.pad(m.reshape(-1, m.shape[-1]), ((0, 0), (0, cols - m.shape[-1])))
+            for m in members
+        ]
+    )
+    flat = jnp.pad(flat, ((0, -flat.shape[0] % 8), (0, 0)))
     grads = [piece for layer in range(layers) for piece in shard_grads[layer]]
-    gate_g, inner_g, extra_g, mixer_g, flat = reduce_grads(grads, flat)
-    flat = flat.reshape(-1)
-    summed, start = [], 0
-    for m in members:
-        summed.append(flat[start : start + m.size].reshape(m.shape))
-        start += m.size
+    gate_g, inner_g, state_g, mixer_g, step_g, *summed = reduce_grads(
+        grads, flat, [m.shape for m in members], 2 * state_size, heads_local
+    )
     return (
         output,
         back,
         summed[0],
         gate_g,
         inner_g,
-        extra_g[:, :, : 2 * state_size],
-        extra_g[:, :, 2 * state_size : 2 * state_size + heads_local],
+        state_g,
+        step_g,
         summed[1],
         summed[2],
         summed[3],
@@ -1051,6 +1114,7 @@
     length, rows, cols = args[0].shape[0], args[4].shape[1], args[4].shape[2]
     heads, states = args[7].shape[2], args[6].shape[2]
     fits = ny == 2 and nz <= 4 and n > 1 and rows % 16 == 0 and cols % 128 == 0
+    fits = fits and max(args[3].shape[1] // n, states) <= cols
     fits = fits and length % (16 * n) == 0 and length == SPAN and cols >= states + heads
     return (body_kernels if fits else body)(*args)
 

time: 350 us -> 339 us (0.969)
  other arithmetic: 37.2 us -> 25.7 us
  local copies, waits for them, and re-layouts: 35.3 us -> 39.5 us
    unnamed x183 -> x193, local copies, waits for them, and re-layouts: 6.62 us -> 24.2 us
    pallas_call x6 -> x4, Pallas kernels: 56.1 us -> 40 us  [tp_sum(): pl.pallas_call(functools.partial(sum_kernel, n, tallied), out_shape=shape...]
    pallas_call x4 -> x6, Pallas kernels: 17.8 us -> 30.8 us  [the longest x2 13.2 us: share_sum(): pl.pallas_call(functools.partial(share_kernel, n), out_shape=jax.ShapeDty...]
    convert_element_type x10 -> x0, other arithmetic: 11.7 us -> none  [the longest x4 5.49 us: body_kernels(): incoming = passed_along(produced.astype(bf), 'ctx', 1).astype(jnp.float32)]
    slice x9 -> x0, local copies, waits for them, and re-layouts: 7.71 us -> none  [the longest x7 5.12 us: body_kernels(): summed.append(flat[start:start + m.size].reshape(m.shape))]
    reshape x17 -> x3, local copies, waits for them, and re-layouts: 6.03 us -> 0.14 us  [the longest x9 5.56 us: body_kernels(): summed.append(flat[start:start + m.size].reshape(m.shape))]
  transfers between devices with their start and end apart: 8 -> 8, of which waited for: 5 -> 6; matrix products, arithmetic and copies ran while one was open for 6% -> 7% of each run, Pallas kernels for 0% -> 0%
where the time goes in v3:
time: 339 us; the launch traced here: 337 us
  Pallas kernels  213 us (63%)
  local copies, waits for them, and re-layouts  39.5 us (12%)
  matrix products  27 us (8%)
  other arithmetic  25.7 us (8%)
  starting transfers between devices  16.8 us (5%)
  waiting for transfers between devices  11.2 us (3%)
  between operations  3.47 us (1%)
    pallas_call x1, Pallas kernels, reduce_grads(): pl.pallas_call(functools.partial(grads_kernel, nz, layers), out_shape=tup...  73.2 us
    pallas_call x1, Pallas kernels, gather_weights(): pl.pallas_call(functools.partial(weights_kernel, nz, ny), out_shape=(jax....  69.3 us
    pallas_call x4, Pallas kernels, tp_sum(): pl.pallas_call(functools.partial(sum_kernel, n, tallied), out_shape=shape...  40 us
    unnamed x193, local copies, waits for them, and re-layouts  24.2 us
    ppermute x8, starting transfers between devices, passed_along(): return lax.ppermute(block, axis, route)  16.8 us
    pallas_call x2, Pallas kernels, share_sum(): pl.pallas_call(functools.partial(share_kernel, n), out_shape=jax.ShapeDty...  13.2 us
    pallas_call x2, Pallas kernels, scan_backward(): pl.pallas_call(back_kernel, out_shape=(f32(length, width), jax.ShapeDtype...  11.3 us
    ppermute x8, waiting for transfers between devices, passed_along(): return lax.ppermute(block, axis, route)  11.2 us
  transfers between devices with their start and end apart: 8, of which 6 were waited for; matrix products, arithmetic and copies ran while one was open for 7% of the time, Pallas kernels for 0%

profile of v3, /device:TPU:0, one launch (start us, length us, event | category | flops | bytes accessed | tf_op | source)
XLA Modules:
  0.0 337.0 jit_solution(13185332807872357275)
XLA Ops:
  2.2 1.0 multiply_reduce_fusion.3
  3.9 1.6 maximum_maximum_fusion.refs_2_
  5.6 69.3 %weights.1 = (bf16[2,768,1152]{2,1,0:T(8,128)(2,1)}, bf16[2,768,384]{2,1,0:T(8,128)(2,1)}) custom-call(bf16[2,96,384]{2,1,0:T(8,128)(2,1)} %refs_0_.1, bf16[2,96,384]{2,1,0:T(8,128)(2,1)} %refs_1_.1, bf16[2,96,384]{2,1,0:T(8,128)(2,1)} %maximum_maximum_fusion.refs_2_, bf16[2,96,384]{2,1,0:T(8,128)(2,1)} %refs_3_.1), custom_call_target="tpu_custom_call" | custom-call | tf_op jit(solution)/shard_map/weights/pallas_call | solution.py:242
  74.9 2.1 fusion.96
  77.1 1.5 collective-permute-start
  89.8 3.2 scan_forward.2
  93.0 1.3 collective-permute-start.1
  94.3 0.9 copy.70
  95.4 1.4 collective-permute-done.1.enter_ref
  96.8 1.9 multiply_reduce_fusion.15
  98.7 1.0 convolution_convert_fusion.5.refs_0_
  100.3 10.5 %tpsum.4 = (bf16[128,768]{1,0:T(8,128)(2,1)}, f32[8,128]{1,0:T(8,128)}) custom-call(bf16[128,768]{1,0:T(8,128)(2,1)} %convolution_convert_fusion.5.refs_0_, f32[8,128]{1,0:T(8,128)} %broadcast_in_dim.24.refs_1_), custom_call_target="tpu_custom_call" | custom-call | tf_op jit(solution)/shard_map/tpsum/pallas_call | solution.py:502
  111.5 1.2 multiply_reduce_fusion.2
  112.7 1.9 fusion.97
  114.7 4.2 %collective-permute-start.2 = (bf16[3,640]{1,0:T(4,128)(2,1)S(1)}, bf16[3,640]{1,0:T(4,128)(2,1)S(1)}, u32[]{:S(2)}, u32[]{:S(2)}) collective-permute-start(bf16[3,640]{1,0:T(4,128)(2,1)S(1)} %slice.413), channel_id=1, source_target_pairs={{0,4},{1,5},{2,6},{3,7},{8,12},{9,13},{10,14},{11,15},{16,20},{17,... | collective-permute-start | bytes 11528 | tf_op jit(solution)/shard_map/ppermute | solution.py:20
  122.1 3.2 scan_forward.3
  125.3 4.2 %collective-permute-start.3 = (bf16[384,128]{1,0:T(8,128)(2,1)}, bf16[384,128]{1,0:T(8,128)(2,1)S(1)}, u32[]{:S(2)}, u32[]{:S(2)}) collective-permute-start(bf16[384,128]{1,0:T(8,128)(2,1)} %get-tuple-element.61), channel_id=1, source_target_pairs={{0,4},{1,5},{2,6},{3,7},{8,12},{9,13},{10,14},{11,15},{16,20},{17,... | collective-permute-start | bytes 294920 | tf_op jit(solution)/shard_map/ppermute | solution.py:20
  130.3 0.9 copy.74
  132.0 2.0 multiply_reduce_fusion.14
  134.7 2.1 convolution_convert_fusion.4.refs_0_
  137.4 9.6 %tpsum.5 = (bf16[128,768]{1,0:T(8,128)(2,1)}, f32[8,128]{1,0:T(8,128)}) custom-call(bf16[128,768]{1,0:T(8,128)(2,1)} %convolution_convert_fusion.4.refs_0_, f32[8,128]{1,0:T(8,128)} %broadcast_in_dim.27.refs_1_), custom_call_target="tpu_custom_call" | custom-call | tf_op jit(solution)/shard_map/tpsum/pallas_call | solution.py:502
  147.7 1.1 multiply_reduce_fusion.1
  149.5 1.6 multiply_multiply_fusion.7
  151.6 1.5 collective-permute-start.4
  153.2 1.2 fusion.12.refs_3_
  155.7 3.1 collective-permute-done.4.leave_ref
  159.5 5.6 %scan_backward.2 = (f32[128,384]{1,0:T(8,128)}, bf16[128,256]{1,0:T(8,128)(2,1)}, f32[128,6]{1,0:T(8,128)}, f32[1,6]{1,0:T(1,128)}, f32[1,384]{1,0:T(1,128)}) custom-call(f32[128,384]{1,0:T(8,128)} %slice.423.x_ref, f32[128,256]{1,0:T(8,128)} %slice.424.bc_ref, f32[128,6]{1,0:T(8,128)} %get-tuple-element.175.step_ref, f32[128,6]{1,0:T(8,128)} %copy-done.5, ...), custom_call_target="tpu_custom_call" | custom-call | tf_op jit(solution)/shard_map/scan_backward/pallas_call | solution.py:620
  165.1 6.6 %share.2 = f32[128,256]{1,0:T(8,128)} custom-call(bf16[128,256]{1,0:T(8,128)(2,1)} %get-tuple-element.65.x), custom_call_target="tpu_custom_call" | custom-call | tf_op jit(solution)/shard_map/share/pallas_call | solution.py:479
  171.7 1.4 multiply_reduce_fusion.7
  173.5 1.3 collective-permute-start.5
  174.8 1.5 fusion.89
  179.4 2.8 fusion.16.refs_0_
  182.3 10.4 %tpsum.6 = bf16[128,768]{1,0:T(8,128)(2,1)} custom-call(bf16[128,768]{1,0:T(8,128)(2,1)} %fusion.16.refs_0_), custom_call_target="tpu_custom_call" | custom-call | tf_op jit(solution)/shard_map/tpsum/pallas_call | solution.py:502
  192.7 1.2 fusion.35
  194.0 1.2 fusion.34
  195.9 1.3 multiply_multiply_fusion.6
  197.7 1.5 collective-permute-start.6
  199.3 2.0 convolution_convert_fusion.refs_2_
  201.2 1.2 convolution_convert_fusion.3.refs_1_
  202.5 2.3 collective-permute-done.6.leave_ref
  205.5 5.6 %scan_backward.3 = (f32[128,384]{1,0:T(8,128)}, bf16[128,256]{1,0:T(8,128)(2,1)}, f32[128,6]{1,0:T(8,128)}, f32[1,6]{1,0:T(1,128)}, f32[1,384]{1,0:T(1,128)}) custom-call(f32[128,384]{1,0:T(8,128)} %slice.406.x_ref, f32[128,256]{1,0:T(8,128)} %slice.407.bc_ref, f32[128,6]{1,0:T(8,128)} %get-tuple-element.183.step_ref, f32[128,6]{1,0:T(8,128)} %copy-done.4, ...), custom_call_target="tpu_custom_call" | custom-call | tf_op jit(solution)/shard_map/scan_backward/pallas_call | solution.py:620
  211.1 6.6 %share.3 = f32[128,256]{1,0:T(8,128)} custom-call(bf16[128,256]{1,0:T(8,128)(2,1)} %get-tuple-element.68.x), custom_call_target="tpu_custom_call" | custom-call | tf_op jit(solution)/shard_map/share/pallas_call | solution.py:479
  217.8 1.4 multiply_reduce_fusion.11
  220.0 1.3 collective-permute-start.7
  222.7 2.9 collective-permute-done.7
  225.9 2.8 fusion.13.refs_0_
  228.7 9.4 %tpsum.7 = bf16[128,768]{1,0:T(8,128)(2,1)} custom-call(bf16[128,768]{1,0:T(8,128)(2,1)} %fusion.13.refs_0_), custom_call_target="tpu_custom_call" | custom-call | tf_op jit(solution)/shard_map/tpsum/pallas_call | solution.py:502
  238.2 1.1 fusion.36
  239.3 1.3 fusion.48
  242.2 2.0 convolution_convert_fusion.1.refs_0_
  245.1 73.2 %grads.1 = (f32[2,96,384]{2,1,0:T(8,128)}, f32[2,96,384]{2,1,0:T(8,128)}, f32[2,96,256]{2,1,0:T(8,128)}, f32[2,96,384]{2,1,0:T(8,128)}, f32[2,96,6]{2,1,0:T(8,12...) custom-call(bf16[768,1152]{1,0:T(8,128)(2,1)} %convolution_convert_f, ...), custom_call_target="tpu_custom_call" | custom-call | tf_op jit(solution)/shard_map/grads/pallas_call | solution.py:377
  318.3 1.6 copy.86
  319.9 1.2 copy.102
  321.2 1.7 copy.103
  322.9 1.7 copy.104
  324.6 1.6 copy.105
  326.2 1.3 copy.106
  327.5 1.3 copy.107
  328.7 1.3 copy.108
  330.0 1.3 copy.109
  331.3 1.2 copy.110
  332.5 1.2 copy.111
  333.8 1.2 copy.112
  335.0 1.3 copy.113
  (309 shorter events, 34.1 us)
Async XLA Ops:
  3.9 73.2 %copy-start.52 = (f32[128]{0:T(128)}, f32[128]{0:T(128)S(1)}, u32[]{:S(2)}) copy-start(f32[128]{0:T(128)S(1)} %fusion.78) | copy-start | bytes 1540
  5.5 73.0 %copy-start.79 = (s32[1,256]{1,0:T(1,128)S(1)}, s32[1,256]{1,0:T(1,128)}, u32[]{:S(2)}) copy-start(s32[1,256]{1,0:T(1,128)} %param.18) | copy-start | bytes 3076
  5.5 74.4 %copy-start.54 = (f32[2,4,256]{2,1,0:T(4,128)S(1)}, f32[2,4,256]{2,1,0:T(4,128)}, u32[]{:S(2)}) copy-start(f32[2,4,256]{2,1,0:T(4,128)} %param.27) | copy-start | bytes 24580
  5.5 74.4 %copy-start.51 = (f32[2,4,384]{2,1,0:T(4,128)S(1)}, f32[2,4,384]{2,1,0:T(4,128)}, u32[]{:S(2)}) copy-start(f32[2,4,384]{2,1,0:T(4,128)} %param.25) | copy-start | bytes 36868
  5.5 75.1 %copy-start.76 = (f32[2,256]{1,0:T(2,128)S(1)}, f32[2,256]{1,0:T(2,128)}, u32[]{:S(2)}) copy-start(f32[2,256]{1,0:T(2,128)} %param.28) | copy-start | bytes 6148
  5.5 75.1 %copy-start.67 = (f32[2,384]{1,0:T(2,128)S(1)}, f32[2,384]{1,0:T(2,128)}, u32[]{:S(2)}) copy-start(f32[2,384]{1,0:T(2,128)} %param.26) | copy-start | bytes 9220
  5.6 75.2 %copy-start.64 = (f32[2,6]{1,0:T(2,128)S(1)}, f32[2,6]{1,0:T(2,128)}, u32[]{:S(2)}) copy-start(f32[2,6]{1,0:T(2,128)} %param.30) | copy-start | bytes 148
  5.6 75.8 %copy-start.80 = (f32[2,6]{1,0:T(2,128)S(1)}, f32[2,6]{1,0:T(2,128)}, u32[]{:S(2)}) copy-start(f32[2,6]{1,0:T(2,128)} %param.29) | copy-start | bytes 148
  74.9 8.8 %copy-start.81 = (f32[2,6]{1,0:T(2,128)S(1)}, f32[2,6]{1,0:T(2,128)}, u32[]{:S(2)}) copy-start(f32[2,6]{1,0:T(2,128)} %param.31) | copy-start | bytes 148
  74.9 8.8 %copy-start.68 = (f32[2,384]{1,0:T(2,128)S(1)}, f32[2,384]{1,0:T(2,128)}, u32[]{:S(2)}) copy-start(f32[2,384]{1,0:T(2,128)} %param.32) | copy-start | bytes 9220
  77.0 19.7 %copy-start.7 = (f32[128,1152]{1,0:T(8,128)}, f32[128,1152]{1,0:T(8,128)S(1)}, u32[]{:S(2)}) copy-start(f32[128,1152]{1,0:T(8,128)S(1)} %get-tuple-element.227) | copy-start | bytes 1769476
  77.1 10.9 %collective-permute-start = (bf16[3,640]{1,0:T(4,128)(2,1)S(1)}, bf16[3,640]{1,0:T(4,128)(2,1)S(1)}, u32[]{:S(2)}, u32[]{:S(2)}) collective-permute-start(bf16[3,640]{1,0:T(4,128)(2,1)S(1)} %slice.396), channel_id=1, source_target_pairs={{0,4},{1,5},{2,6},{3,7},{8,12},{9,13},{10,14},{11,15},{16,20},{17,... | collective-permute-start | bytes 11528 | tf_op jit(solution)/shard_map/ppermute | solution.py:20
  80.6 39.7 %copy-start.33 = (f32[128]{0:T(128)}, f32[128]{0:T(128)S(1)}, u32[]{:S(2)}) copy-start(f32[128]{0:T(128)S(1)} %get-tuple-element.223) | copy-start | bytes 1540
  80.7 39.7 %copy-start.36 = (f32[128]{0:T(128)}, f32[128]{0:T(128)S(1)}, u32[]{:S(2)}) copy-start(f32[128]{0:T(128)S(1)} %get-tuple-element.224) | copy-start | bytes 1540
  80.7 39.7 %copy-start.39 = (f32[128]{0:T(128)}, f32[128]{0:T(128)S(1)}, u32[]{:S(2)}) copy-start(f32[128]{0:T(128)S(1)} %get-tuple-element.225) | copy-start | bytes 1540
  81.9 6.5 %copy-start.60 = (f32[6]{0:T(128)}, f32[6]{0:T(128)S(1)}, u32[]{:S(2)}) copy-start(f32[6]{0:T(128)S(1)} %get-tuple-element.216) | copy-start | bytes 76
  84.3 14.4 %copy-start.48 = (f32[384]{0:T(512)}, f32[384]{0:T(512)S(1)}, u32[]{:S(2)}) copy-start(f32[384]{0:T(512)S(1)} %get-tuple-element.161) | copy-start | bytes 4612
  87.9 32.5 %copy-start.26 = (f32[640]{0:T(1024)}, f32[640]{0:T(1024)S(1)}, u32[]{:S(2)}) copy-start(f32[640]{0:T(1024)S(1)} %get-tuple-element.151) | copy-start | bytes 7684
  88.0 32.5 %copy-start.28 = (f32[640]{0:T(1024)}, f32[640]{0:T(1024)S(1)}, u32[]{:S(2)}) copy-start(f32[640]{0:T(1024)S(1)} %get-tuple-element.152) | copy-start | bytes 7684
  88.0 32.5 %copy-start.30 = (f32[640]{0:T(1024)}, f32[640]{0:T(1024)S(1)}, u32[]{:S(2)}) copy-start(f32[640]{0:T(1024)S(1)} %get-tuple-element.153) | copy-start | bytes 7684
  88.4 10.3 %copy-start.2 = (bf16[2,768,384]{2,1,0:T(8,128)(2,1)S(1)}, bf16[2,768,384]{2,1,0:T(8,128)(2,1)}, u32[]{:S(2)}) copy-start(bf16[2,768,384]{2,1,0:T(8,128)(2,1)} %get-tuple-element.56) | copy-start | bytes 3538948
  89.8 21.7 %copy-start = (bf16[128,768]{1,0:T(8,128)(2,1)S(1)}, bf16[128,768]{1,0:T(8,128)(2,1)}, u32[]{:S(2)}) copy-start(bf16[128,768]{1,0:T(8,128)(2,1)} %param.17) | copy-start | bytes 589828
  93.0 3.8 %collective-permute-start.1 = (bf16[384,128]{1,0:T(8,128)(2,1)}, bf16[384,128]{1,0:T(8,128)(2,1)S(1)}, u32[]{:S(2)}, u32[]{:S(2)}) collective-permute-start(bf16[384,128]{1,0:T(8,128)(2,1)} %get-tuple-element.55), channel_id=1, source_target_pairs={{0,4},{1,5},{2,6},{3,7},{8,12},{9,13},{10,14},{11,15},{16,20},{17,... | collective-permute-start | bytes 294920 | tf_op jit(solution)/shard_map/ppermute | solution.py:20
  95.4 16.1 %copy-start.8 = (f32[128,384]{1,0:T(8,128)}, f32[128,384]{1,0:T(8,128)S(1)}, u32[]{:S(2)}) copy-start(f32[128,384]{1,0:T(8,128)S(1)} %copy.71) | copy-start | bytes 589828
  96.8 17.9 %copy-start.20 = (bf16[384,128]{1,0:T(8,128)(2,1)}, bf16[384,128]{1,0:T(8,128)(2,1)S(1)}, u32[]{:S(2)}) copy-start(bf16[384,128]{1,0:T(8,128)(2,1)S(1)} %collective-permute-done.1.enter_ref) | copy-start | bytes 294916
  98.7 12.8 %copy-start.14 = (f32[128,384]{1,0:T(8,128)}, f32[128,384]{1,0:T(8,128)S(1)}, u32[]{:S(2)}) copy-start(f32[128,384]{1,0:T(8,128)S(1)} %get-tuple-element.181) | copy-start | bytes 589828
  111.5 7.4 %copy-start.62 = (f32[6]{0:T(128)S(1)}, f32[6]{0:T(128)}, u32[]{:S(2)}) copy-start(f32[6]{0:T(128)} %get-tuple-element.215) | copy-start | bytes 76
  111.5 7.4 %copy-start.74 = (f32[6]{0:T(128)S(1)}, f32[6]{0:T(128)}, u32[]{:S(2)}) copy-start(f32[6]{0:T(128)} %get-tuple-element.210) | copy-start | bytes 76
  112.7 7.0 %copy-start.84 = (f32[128]{0:T(128)}, f32[128]{0:T(128)S(1)}, u32[]{:S(2)}) copy-start(f32[128]{0:T(128)S(1)} %get-tuple-element.178) | copy-start | bytes 1540
  112.7 7.0 %copy-start.55 = (f32[128]{0:T(128)}, f32[128]{0:T(128)S(1)}, u32[]{:S(2)}) copy-start(f32[128]{0:T(128)S(1)} %fusion.79) | copy-start | bytes 1540
  114.7 5.6 %collective-permute-start.2 = (bf16[3,640]{1,0:T(4,128)(2,1)S(1)}, bf16[3,640]{1,0:T(4,128)(2,1)S(1)}, u32[]{:S(2)}, u32[]{:S(2)}) collective-permute-start(bf16[3,640]{1,0:T(4,128)(2,1)S(1)} %slice.413), channel_id=1, source_target_pairs={{0,4},{1,5},{2,6},{3,7},{8,12},{9,13},{10,14},{11,15},{16,20},{17,... | collective-permute-start | bytes 11528 | tf_op jit(solution)/shard_map/ppermute | solution.py:20
  125.3 22.3 %copy-start.1 = (f32[128,768]{1,0:T(8,128)S(1)}, f32[128,768]{1,0:T(8,128)}, u32[]{:S(2)}) copy-start(f32[128,768]{1,0:T(8,128)} %param.19) | copy-start | bytes 1179652
  125.3 6.7 %collective-permute-start.3 = (bf16[384,128]{1,0:T(8,128)(2,1)}, bf16[384,128]{1,0:T(8,128)(2,1)S(1)}, u32[]{:S(2)}, u32[]{:S(2)}) collective-permute-start(bf16[384,128]{1,0:T(8,128)(2,1)} %get-tuple-element.61), channel_id=1, source_target_pairs={{0,4},{1,5},{2,6},{3,7},{8,12},{9,13},{10,14},{11,15},{16,20},{17,... | collective-permute-start | bytes 294920 | tf_op jit(solution)/shard_map/ppermute | solution.py:20
  131.2 18.3 %copy-start.50 = (f32[384]{0:T(512)S(1)}, f32[384]{0:T(512)}, u32[]{:S(2)}) copy-start(f32[384]{0:T(512)} %get-tuple-element.160) | copy-start | bytes 4612
  132.0 17.4 %copy-start.21 = (bf16[384,128]{1,0:T(8,128)(2,1)}, bf16[384,128]{1,0:T(8,128)(2,1)S(1)}, u32[]{:S(2)}) copy-start(bf16[384,128]{1,0:T(8,128)(2,1)S(1)} %collective-permute-done.3.enter_ref) | copy-start | bytes 294916
  151.1 7.7 %copy-start.13 = (f32[128,384]{1,0:T(8,128)}, f32[128,384]{1,0:T(8,128)S(1)}, u32[]{:S(2)}) copy-start(f32[128,384]{1,0:T(8,128)S(1)} %get-tuple-element.188.dm_ref) | copy-start | bytes 589828
  151.1 20.6 %copy-start.34 = (f32[128]{0:T(128)S(1)}, f32[128]{0:T(128)}, u32[]{:S(2)}) copy-start(f32[128]{0:T(128)} %copy-done.33) | copy-start | bytes 1540
  151.1 20.6 %copy-start.37 = (f32[128]{0:T(128)S(1)}, f32[128]{0:T(128)}, u32[]{:S(2)}) copy-start(f32[128]{0:T(128)} %copy-done.36) | copy-start | bytes 1540
  151.1 20.6 %copy-start.40 = (f32[128]{0:T(128)S(1)}, f32[128]{0:T(128)}, u32[]{:S(2)}) copy-start(f32[128]{0:T(128)} %copy-done.39) | copy-start | bytes 1540
  151.6 7.2 %collective-permute-start.4 = (bf16[384,128]{1,0:T(8,128)(2,1)S(1)}, bf16[384,128]{1,0:T(8,128)(2,1)S(1)}, u32[]{:S(2)}, u32[]{:S(2)}) collective-permute-start(bf16[384,128]{1,0:T(8,128)(2,1)S(1)} %convolution_convert_fusion.7), channel_id=1, source_target_pairs={{4,0},{5,1},{6,2},{7,3},{12,8},{13,9},{14,10},{15,11},{20,16},{21,... | collective-permute-start | bytes 294920 | tf_op jit(solution)/shard_map/ppermute | solution.py:20
  159.5 13.7 %copy-start.27 = (f32[640]{0:T(1024)S(1)}, f32[640]{0:T(1024)}, u32[]{:S(2)}) copy-start(f32[640]{0:T(1024)} %copy-done.26) | copy-start | bytes 7684
  159.5 13.7 %copy-start.29 = (f32[640]{0:T(1024)S(1)}, f32[640]{0:T(1024)}, u32[]{:S(2)}) copy-start(f32[640]{0:T(1024)} %copy-done.28) | copy-start | bytes 7684
  159.5 13.7 %copy-start.31 = (f32[640]{0:T(1024)S(1)}, f32[640]{0:T(1024)}, u32[]{:S(2)}) copy-start(f32[640]{0:T(1024)} %copy-done.30) | copy-start | bytes 7684
  173.5 5.6 %collective-permute-start.5 = (f32[3,640]{1,0:T(4,128)S(1)}, f32[3,640]{1,0:T(4,128)S(1)}, u32[]{:S(2)}, u32[]{:S(2)}) collective-permute-start(f32[3,640]{1,0:T(4,128)S(1)} %pad_add_fusion.3), channel_id=1, source_target_pairs={{4,0},{5,1},{6,2},{7,3},{12,8},{13,9},{14,10},{15,11},{20,16},{21,... | collective-permute-start | bytes 23048 | tf_op jit(solution)/shard_map/ppermute | solution.py:20
  176.3 6.0 %copy-start.42 = (f32[1,640]{1,0:T(1,128)}, f32[1,640]{1,0:T(1,128)S(1)}, u32[]{:S(2)}) copy-start(f32[1,640]{1,0:T(1,128)S(1)} %reshape.229) | copy-start | bytes 7684
  176.3 5.9 %copy-start.44 = (f32[1,640]{1,0:T(1,128)}, f32[1,640]{1,0:T(1,128)S(1)}, u32[]{:S(2)}) copy-start(f32[1,640]{1,0:T(1,128)S(1)} %reshape.228) | copy-start | bytes 7684
  176.3 5.9 %copy-start.46 = (f32[1,640]{1,0:T(1,128)}, f32[1,640]{1,0:T(1,128)S(1)}, u32[]{:S(2)}) copy-start(f32[1,640]{1,0:T(1,128)S(1)} %reshape.227) | copy-start | bytes 7684
  179.2 13.5 %copy-start.56 = (f32[128]{0:T(128)S(1)}, f32[128]{0:T(128)}, u32[]{:S(2)}) copy-start(f32[128]{0:T(128)} %copy-done.55) | copy-start | bytes 1540
  179.3 14.6 %copy-start.85 = (f32[128]{0:T(128)S(1)}, f32[128]{0:T(128)}, u32[]{:S(2)}) copy-start(f32[128]{0:T(128)} %copy-done.84) | copy-start | bytes 1540
  179.4 14.6 %copy-start.10 = (bf16[128,768]{1,0:T(8,128)(2,1)S(1)}, bf16[128,768]{1,0:T(8,128)(2,1)}, u32[]{:S(2)}) copy-start(bf16[128,768]{1,0:T(8,128)(2,1)} %get-tuple-element.57) | copy-start | bytes 589828
  182.2 13.7 %copy-start.15 = (f32[128,384]{1,0:T(8,128)S(1)}, f32[128,384]{1,0:T(8,128)}, u32[]{:S(2)}) copy-start(f32[128,384]{1,0:T(8,128)} %copy-done.14) | copy-start | bytes 589828
  182.2 13.7 %copy-start.19 = (f32[128,384]{1,0:T(8,128)S(1)}, f32[128,384]{1,0:T(8,128)}, u32[]{:S(2)}) copy-start(f32[128,384]{1,0:T(8,128)} %get-tuple-element.228.mixed_ref) | copy-start | bytes 589828
  182.2 13.7 %copy-start.49 = (f32[384]{0:T(512)S(1)}, f32[384]{0:T(512)}, u32[]{:S(2)}) copy-start(f32[384]{0:T(512)} %copy-done.48) | copy-start | bytes 4612
  182.3 13.7 %copy-start.72 = (f32[128]{0:T(128)S(1)}, f32[128]{0:T(128)}, u32[]{:S(2)}) copy-start(f32[128]{0:T(128)} %copy-done.71) | copy-start | bytes 1540
  197.7 7.1 %collective-permute-start.6 = (bf16[384,128]{1,0:T(8,128)(2,1)S(1)}, bf16[384,128]{1,0:T(8,128)(2,1)S(1)}, u32[]{:S(2)}, u32[]{:S(2)}) collective-permute-start(bf16[384,128]{1,0:T(8,128)(2,1)S(1)} %convolution_convert_fusion.6), channel_id=1, source_target_pairs={{4,0},{5,1},{6,2},{7,3},{12,8},{13,9},{14,10},{15,11},{20,16},{21,... | collective-permute-start | bytes 294920 | tf_op jit(solution)/shard_map/ppermute | solution.py:20
  201.2 16.5 %copy-start.35 = (f32[128]{0:T(128)S(1)}, f32[128]{0:T(128)}, u32[]{:S(2)}) copy-start(f32[128]{0:T(128)} %copy-done.33) | copy-start | bytes 1540
  201.2 16.5 %copy-start.38 = (f32[128]{0:T(128)S(1)}, f32[128]{0:T(128)}, u32[]{:S(2)}) copy-start(f32[128]{0:T(128)} %copy-done.36) | copy-start | bytes 1540
  201.2 16.5 %copy-start.41 = (f32[128]{0:T(128)S(1)}, f32[128]{0:T(128)}, u32[]{:S(2)}) copy-start(f32[128]{0:T(128)} %copy-done.39) | copy-start | bytes 1540
  220.0 5.6 %collective-permute-start.7 = (f32[3,640]{1,0:T(4,128)S(1)}, f32[3,640]{1,0:T(4,128)S(1)}, u32[]{:S(2)}, u32[]{:S(2)}) collective-permute-start(f32[3,640]{1,0:T(4,128)S(1)} %pad_add_fusion.2), channel_id=1, source_target_pairs={{4,0},{5,1},{6,2},{7,3},{12,8},{13,9},{14,10},{15,11},{20,16},{21,... | collective-permute-start | bytes 23048 | tf_op jit(solution)/shard_map/ppermute | solution.py:20
  222.6 6.1 %copy-start.57 = (f32[1,640]{1,0:T(1,128)}, f32[1,640]{1,0:T(1,128)S(1)}, u32[]{:S(2)}) copy-start(f32[1,640]{1,0:T(1,128)S(1)} %reshape.232) | copy-start | bytes 7684
  225.8 12.4 %copy-start.53 = (f32[128]{0:T(128)S(1)}, f32[128]{0:T(128)}, u32[]{:S(2)}) copy-start(f32[128]{0:T(128)} %copy-done.52) | copy-start | bytes 1540
  225.9 13.4 %copy-start.83 = (f32[128]{0:T(128)S(1)}, f32[128]{0:T(128)}, u32[]{:S(2)}) copy-start(f32[128]{0:T(128)} %copy-done.82) | copy-start | bytes 1540
  225.9 13.4 %copy-start.70 = (f32[128]{0:T(128)S(1)}, f32[128]{0:T(128)}, u32[]{:S(2)}) copy-start(f32[128]{0:T(128)} %copy-done.69) | copy-start | bytes 1540
  318.3 17.9 %copy-start.18 = (f32[2,96,384]{2,1,0:T(8,128)S(1)}, f32[2,96,384]{2,1,0:T(8,128)}, u32[]{:S(2)}) copy-start(f32[2,96,384]{2,1,0:T(8,128)} %get-tuple-element.277) | copy-start | bytes 884740
  (34 other events, 98.2 us)
